TPU v7x, 32 devices: a whole 2x2x4 slice. The times are simulated.
32 devices in a mesh: group: 4 (over y, core), member: 8 (over z, x).
Axes of the slice: x: 2, y: 2, z: 4, core: 2. Of those that a mesh axis runs over, the one named last changes fastest.
Arguments:
- tokens: bfloat16 [128, 196, 768], P(('group', 'member')), may hold values from -6 to 6
- w_query: bfloat16 [768, 768], replicated, may hold values from -8 to 8
- w_key: bfloat16 [768, 768], replicated, may hold values from -1 to 1
- w_value: bfloat16 [768, 768], replicated, may hold values from -0.21875 to 0.21875
- w_out: bfloat16 [768, 768], replicated, may hold values from -0.21875 to 0.21875
- partners: int32 [128, 4], P(('group', 'member')), may hold values from 0 to 127, as said below
- counts: int32 [128], P(('group', 'member')), may hold values from 1 to 4
- key_slot: int32 [32], P(('group', 'member')), may hold values from 0 to 3
Outputs:
- refined: bfloat16 [128, 196, 768], P(('group', 'member'))
Inputs may be any that keep to these rules, and one draw needn't show every extreme that they name: `partners`: every entry names a view held by another device of the same group; the entries of all views of one device name views of one other device at most 3 times, and those of some other device exactly 3 times.
All inputs are finite; a program needn't handle non-finite values.
Results may differ from a plain program's by a relative error of at most 0.011.
Values may be sent and summed in bfloat16 or wider, within the bound.
A program may use at most 128 MiB of HBM per device.

v0:
```python
import functools

import jax
import jax.numpy as jnp
from jax import lax
from jax.experimental import pallas as pl
from jax.experimental.pallas import tpu as pltpu
from jax.sharding import PartitionSpec as P

HEADS = 12
ROW = 2
LAYERS = 4
MESH = pl.DeviceIdType.MESH


def layer_norm(values_in):
    values_in = values_in.astype(jnp.float32)
    centre = jnp.mean(values_in, axis=-1, keepdims=True)
    spread = jnp.mean((values_in - centre) ** 2, axis=-1, keepdims=True)
    return (values_in - centre) * lax.rsqrt(spread + 1e-05)


def project(rows, weights):
    return jnp.dot(rows, weights, preferred_element_type=jnp.float32)


def attend(query, normed, w_key, w_value, pair, store):
    features = normed.shape[1]
    size = features // HEADS
    lower = lax.broadcasted_iota(jnp.int32, (1, 2 * size), 1) < size
    pair[:, :features] = project(normed, w_key[...]).astype(jnp.bfloat16)
    pair[:, features:] = project(normed, w_value[...]).astype(jnp.bfloat16)
    for h in range(HEADS // 2):
        cols = pl.ds(2 * h * size, 2 * size)
        rows = query(cols)
        key = pair[:, cols]
        value = pair[:, pl.ds(features + 2 * h * size, 2 * size)]
        halves = []
        for keep in (lower, jnp.logical_not(lower)):
            part = jnp.where(keep, rows, jnp.zeros_like(rows))
            scores = lax.dot_general(
                part, key, (((1,), (1,)), ((), ())), preferred_element_type=jnp.float32
            )
            top = jnp.max(scores, axis=-1, keepdims=True)
            weights = jnp.exp(scores - top)
            mass = jnp.sum(weights, axis=-1, keepdims=True)
            halves.append(project(weights.astype(jnp.bfloat16), value) / mass)
        store(cols, jnp.where(lower, halves[0], halves[1]))


def sublayer_kernel(degree, capacity, *refs):
    table, ask, weight, key_weight, tokens_in, wq_in, wk_in, wv_in, wo_in, out_ref = refs[:10]
    tokens, w_query, w_key, w_value, w_out = refs[10:15]
    own, queries, near, b0, b1, b2, s0, s1, s2, keys, staged, key_out = refs[15:27]
    asked, cur, pair, results, load_sem, send_sem, recv_sem = refs[27:]
    views, length, features = tokens.shape
    members, groups = lax.axis_size("member"), lax.axis_size("group")
    entries = views * degree
    peers = members - 1
    size = features // HEADS
    me, group = lax.axis_index("member"), lax.axis_index("group")
    layer, side = me // ROW, me % ROW
    low = layer < LAYERS // 2
    toward = jnp.where(low, ROW, -ROW)
    is_end = jnp.logical_or(layer == 0, layer == LAYERS - 1)
    is_mid = jnp.logical_not(is_end)
    beside = {"member": layer * ROW + 1 - side}
    inner = {"member": me + toward}
    outer = {"member": jnp.clip(me - toward, 0, members - 1)}
    above = {"group": lax.rem(group + 1, groups)}
    below = {"group": lax.rem(group + groups - 1, groups)}

    blocks = (near, b0, s0, b1, s1, b2, s2)
    base, total = {}, 0
    for name, ref in (("near", near), ("b0", b0), ("b1", b1), ("b2", b2), ("s0", s0),
                      ("s1", s1), ("s2", s2), ("keys", keys)):
        base[name] = total
        total += ref.shape[0]

    def remote(source, target, send, recv, device):
        return pltpu.make_async_remote_copy(
            src_ref=source, dst_ref=target, send_sem=send_sem.at[send],
            recv_sem=recv_sem.at[recv], device_id=device, device_id_type=MESH,
        )

    sends = {}

    def slot(name, index):
        return sends.setdefault((name, index), len(sends))

    def hop(name, source, v, target, target_name, device):
        return remote(source.at[v], target.at[v], slot(name, v), base[target_name] + v, device)

    def to_near(v):
        return hop("near", own, v, near, "near", beside)

    def own_to_b1(v):
        return hop("in", own, v, b1, "b1", inner)

    def own_to_b0(v):
        return hop("in", own, v, b0, "b0", inner)

    def own_out(v):
        return hop("out", own, v, b0, "b0", outer)

    def b1_in(v):
        return hop("in2", b1, v, b2, "b2", inner)

    def b0_out(v):
        return hop("out1", b0, v, b1, "b1", outer)

    def b2_out(v):
        return hop("out2", b2, v, b2, "b2", outer)

    swaps = (s0, s1, s2)

    def swap(j, k):
        return remote(
            staged.at[j * capacity + k], swaps[j].at[k], slot("swap", j * capacity + k),
            base[f"s{j}"] + k, beside,
        )

    def key_send(i):
        return remote(
            key_out, keys.at[i], slot("key", i), base["keys"] + i, above if i == 0 else below
        )

    def ask_send():
        return remote(ask, asked, slot("ask", 0), total, beside)

    loads = [
        pltpu.make_async_copy(source, target, load_sem.at[i])
        for i, (source, target) in enumerate(
            ((tokens_in, tokens), (wq_in, w_query), (wk_in, w_key), (wv_in, w_value), (wo_in, w_out))
        )
    ]
    for load in loads:
        load.start()

    barrier = pltpu.get_barrier_semaphore()
    for device in (beside, inner, above, below):
        pl.semaphore_signal(barrier, inc=1, device_id=device, device_id_type=MESH)

    @pl.when(is_mid)
    def _():
        pl.semaphore_signal(barrier, inc=1, device_id=outer, device_id_type=MESH)

    loads[0].wait()
    own[0] = layer_norm(tokens[0]).astype(jnp.bfloat16)

    @pl.when(is_mid)
    def _():
        pl.semaphore_wait(barrier, 5)

    @pl.when(is_end)
    def _():
        pl.semaphore_wait(barrier, 4)

    for v in range(views):
        if v:
            own[v] = layer_norm(tokens[v]).astype(jnp.bfloat16)
        to_near(v).start()

        @pl.when(is_end)
        def _():
            own_to_b1(v).start()

        @pl.when(is_mid)
        def _():
            own_to_b0(v).start()
            own_out(v).start()

    ask_send().start()
    key_out[...] = own[table[3, 0]]
    loads[1].wait()
    for v in range(views):
        queries[v] = project(own[v], w_query[...]).astype(jnp.bfloat16) * jnp.bfloat16(size**-0.5)
    for i in range(2):
        key_send(i).start()
    loads[2].wait()
    loads[3].wait()
    for i in range(2):
        key_send(i).wait_recv()

    def stage(j, k, source):
        choice = asked[0, j * capacity + k]
        value = source[0]
        for v in range(1, k + views - capacity + 1):
            value = jnp.where(choice == v, source[v], value)
        staged[j * capacity + k] = value
        swap(j, k).start()

    def events(t):
        def far(v):
            @pl.when(is_end)
            def _():
                b0_out(v).wait_recv()

            @pl.when(is_mid)
            def _():
                b1_in(v).wait_recv()
                b2_out(v).start()

        def last(v):
            @pl.when(is_end)
            def _():
                b2_out(v).wait_recv()

        def arrive(j):
            for k in range(capacity):
                swap(j, k).wait_recv()

        extra = views - capacity

        def spread(wait, j, source, v):
            wait(v)
            if v >= extra:
                stage(j, v - extra, source)

        if t == first[0]:
            for v in range(views):
                own_to_b0(v).wait_recv()

                @pl.when(is_mid)
                def _():
                    b0_out(v).start()
                    own_to_b1(v).wait_recv()
                    b1_in(v).start()

                if v >= extra:
                    stage(0, v - extra, b0)
            for v in range(views):
                to_near(v).wait_recv()
        if t == first[2]:
            for v in range(views - 2):
                spread(far, 1, b1, v)
            arrive(0)
        if t == first[2] + 1:
            spread(far, 1, b1, views - 2)
        if t == first[3]:
            spread(far, 1, b1, views - 1)
        if t == first[4]:
            for v in range(views - 2):
                spread(last, 2, b2, v)
            arrive(1)
        if t == first[4] + 1:
            spread(last, 2, b2, views - 2)
        if t == first[5]:
            spread(last, 2, b2, views - 1)
        if t == first[6]:
            arrive(2)

    first = [2 + max(0, entries - capacity * (peers - j)) for j in range(peers)]

    def entry(t, carry):
        for when in sorted({first[0], first[2], first[2] + 1, first[3], first[4], first[4] + 1,
                            first[5], first[6]}):
            @pl.when(t == when)
            def _():
                events(when)

        @pl.when(t < 2)
        def _():
            cur[...] = keys[jnp.minimum(t, 1)]

        block, place, view = table[0, t], table[1, t], table[2, t]
        for j, ref in enumerate(blocks):
            @pl.when(t >= first[j])
            def _():
                value = ref[jnp.minimum(place, ref.shape[0] - 1)]
                cur[...] = jnp.where(block == j, value, cur[...])

        def store(cols, value):
            results[t, :, cols] = value

        attend(lambda cols: queries[view, :, cols], cur[...], w_key, w_value, pair, store)
        return carry

    ask_send().wait_recv()
    lax.fori_loop(0, entries + 2, entry, 0)
    loads[4].wait()
    for v in range(views):
        mixed = key_weight[v] * (results[0] + results[1])
        for e in range(degree):
            mixed += weight[v * degree + e] * results[table[4, v * degree + e]]
        out_ref[v] = (
            tokens[v].astype(jnp.float32) + project(mixed.astype(jnp.bfloat16), w_out[...])
        ).astype(out_ref.dtype)

    for v in range(views):
        to_near(v).wait_send()

        @pl.when(is_end)
        def _():
            own_to_b1(v).wait_send()

        @pl.when(is_mid)
        def _():
            own_to_b0(v).wait_send()
            own_out(v).wait_send()
            b1_in(v).wait_send()
            b0_out(v).wait_send()
            b2_out(v).wait_send()

    for j in range(3):
        for k in range(capacity):
            swap(j, k).wait_send()
    for i in range(2):
        key_send(i).wait_send()
    ask_send().wait_send()


def one_kernel(tokens, w_query, w_key, w_value, w_out, partners, counts, slot_key):
    views, length, features = tokens.shape
    members = lax.axis_size("member")
    me = lax.axis_index("member")
    degree = partners.shape[1]
    entry_list = partners.reshape(-1)
    entries = entry_list.shape[0]
    capacity = (entries + members - 2) // (members - 1)
    peers = entry_list // views % members
    places = entry_list % views
    layer, side = me // ROW, me % ROW
    ranking = jnp.array([[9, 0, 1, 2], [1, 9, 0, 2], [2, 0, 9, 1], [2, 1, 0, 9]], jnp.int32)[layer]
    layers = jnp.arange(LAYERS, dtype=jnp.int32)
    peer_layer = peers // ROW
    turn = jnp.sum(jnp.where(peer_layer[:, None] == layers[None, :], ranking[None, :], 0), axis=1)
    across = peers % ROW != side
    block = jnp.where(peer_layer == layer, 0, 1 + 2 * turn + across.astype(jnp.int32))
    order = jnp.arange(entries, dtype=jnp.int32)
    code = block * entries + order
    position = jnp.sum((code[None, :] < code[:, None]).astype(jnp.int32), axis=1)
    spots = jnp.arange(views, dtype=jnp.int32)
    turns = jnp.arange(LAYERS - 1, dtype=jnp.int32)
    wanted = jnp.any(
        (block[None, None, :] == 2 + 2 * turns[:, None, None])
        & (places[None, None, :] == spots[None, :, None]),
        axis=2,
    ).astype(jnp.int32)
    before = jnp.sum(
        jnp.where(spots[None, None, :] < spots[None, :, None], wanted[:, None, :], 0), axis=2
    )
    slots = capacity - jnp.sum(wanted, axis=1, keepdims=True) + before
    slot_ids = jnp.arange(capacity, dtype=jnp.int32)
    ask = jnp.sum(
        jnp.where(
            (wanted[:, None, :] == 1) & (slots[:, None, :] == slot_ids[None, :, None]),
            spots[None, None, :],
            0,
        ),
        axis=2,
    ).reshape(1, -1)
    picked = jnp.sum(
        jnp.where(
            (block[:, None, None] == 2 + 2 * turns[None, :, None])
            & (places[:, None, None] == spots[None, None, :]),
            slots[None, :, :],
            0,
        ),
        axis=(1, 2),
    )
    spot = jnp.where((block > 0) & across, picked, places)
    here = position[None, :] == order[:, None]
    data = jnp.stack((block, spot, order // degree))
    data = jnp.sum(jnp.where(here[None], data[:, None, :], 0), axis=2)
    lead = jnp.stack((jnp.full((2,), -1, jnp.int32), jnp.zeros((2,), jnp.int32), jnp.full((2,), slot_key)))
    data = jnp.concatenate((lead, data), axis=1)
    tail = jnp.stack(
        (jnp.full((entries + 2,), slot_key), jnp.concatenate((position + 2, jnp.zeros((2,), jnp.int32))))
    )
    table = jnp.concatenate((data, tail), axis=0)
    is_key = (spots == slot_key).astype(jnp.int32)
    inverse = 1.0 / (counts + 2 * is_key).astype(jnp.float32)
    live = (jnp.arange(degree, dtype=jnp.int32)[None, :] < counts[:, None]).astype(jnp.float32)
    weight = (live * inverse[:, None]).reshape(-1)
    key_weight = is_key.astype(jnp.float32) * inverse

    smem = pl.BlockSpec(memory_space=pltpu.SMEM)
    hbm = pl.BlockSpec(memory_space=pl.ANY)
    slab = (length, features)
    weights_shape = pltpu.VMEM((features, features), jnp.bfloat16)
    half = jnp.bfloat16
    blocks = [pltpu.VMEM((views, *slab), half)] * 6 + [pltpu.VMEM((capacity, *slab), half)] * 3
    sends = 6 * views + 3 * capacity + 3 + views
    receives = 4 * views + 3 * capacity + 3
    return pl.pallas_call(
        functools.partial(sublayer_kernel, degree, capacity),
        out_shape=jax.ShapeDtypeStruct(tokens.shape, tokens.dtype),
        in_specs=[smem] * 4 + [hbm] * 5,
        out_specs=pl.BlockSpec(memory_space=pltpu.VMEM),
        scratch_shapes=[
            pltpu.VMEM(tokens.shape, tokens.dtype),
            weights_shape,
            weights_shape,
            weights_shape,
            weights_shape,
            *blocks,
            pltpu.VMEM((2, *slab), half),
            pltpu.VMEM((3 * capacity, *slab), half),
            pltpu.VMEM(slab, half),
            pltpu.SMEM(ask.shape, jnp.int32),
            pltpu.VMEM(slab, half),
            pltpu.VMEM((length, 2 * features), half),
            pltpu.VMEM((entries + 2, *slab), jnp.float32),
            pltpu.SemaphoreType.DMA((5,)),
            pltpu.SemaphoreType.DMA((sends,)),
            pltpu.SemaphoreType.DMA((receives,)),
        ],
        compiler_params=pltpu.CompilerParams(
            collective_id=0, has_side_effects=True, vmem_limit_bytes=60 * 1024 * 1024
        ),
        name="sublayer",
    )(table, ask, weight, key_weight, tokens, w_query, w_key, w_value, w_out)


def local_kernel(table, queries, w_key, w_value, block, inverse, tokens, w_out, out_ref, *scratch):
    held, pair, total, sem = scratch
    copy = pltpu.make_async_copy(block, held, sem)
    copy.start()
    total[...] = jnp.zeros_like(total)
    copy.wait()
    views, length, _ = total.shape

    def entry(e, carry):
        @pl.when(table[0, e] == 1)
        def _():
            place, view = table[1, e], table[2, e]

            def store(cols, value):
                total[view, :, cols] += value

            normed = layer_norm(held[place]).astype(jnp.bfloat16)
            attend(lambda cols: queries[view, :, cols], normed, w_key, w_value, pair, store)

        return carry

    lax.fori_loop(0, table.shape[1], entry, 0)
    for v in range(views):
        mixed = (total[v] * inverse[v]).astype(jnp.bfloat16)
        out_ref[v] = (tokens[v].astype(jnp.float32) + project(mixed, w_out[...])).astype(out_ref.dtype)


def exchange(tokens, w_query, w_key, w_value, w_out, partners, counts, slot_key):
    views, length, features = tokens.shape
    members, groups = lax.axis_size("member"), lax.axis_size("group")
    degree = partners.shape[1]
    entry_list = partners.reshape(-1)
    entries = entry_list.shape[0]
    capacity = (entries + members - 2) // (members - 1)
    peers = entry_list // views % members
    places = entry_list % views
    order = jnp.arange(entries, dtype=jnp.int32)
    earlier = (peers[:, None] == peers[None, :]) & (order[None, :] < order[:, None])
    cells = peers * capacity + jnp.sum(earlier.astype(jnp.int32), axis=1)
    requests = jnp.zeros((members * capacity,), jnp.int32).at[cells].set(places)
    asked = lax.all_to_all(
        requests.reshape(members, capacity), "member", split_axis=0, concat_axis=0, tiled=True
    )
    outgoing = tokens[asked.reshape(-1)].reshape(members, capacity, length, features)
    arrived = lax.all_to_all(outgoing, "member", split_axis=0, concat_axis=0, tiled=True)
    own_key = lax.dynamic_slice_in_dim(tokens, slot_key, 1, 0)
    below = lax.ppermute(own_key, "group", [(g, (g + 1) % groups) for g in range(groups)])
    above = lax.ppermute(own_key, "group", [((g + 1) % groups, g) for g in range(groups)])
    block = jnp.concatenate((arrived.reshape(members * capacity, length, features), below, above))
    normed = layer_norm(tokens).astype(jnp.bfloat16)
    queries = project(normed.reshape(views * length, features), w_query).astype(jnp.bfloat16)
    queries = queries.reshape(tokens.shape) * jnp.bfloat16((features // HEADS) ** -0.5)
    is_key = (jnp.arange(views, dtype=jnp.int32) == slot_key).astype(jnp.int32)
    inverse = 1.0 / (counts + 2 * is_key).astype(jnp.float32)
    live = (jnp.arange(degree, dtype=jnp.int32)[None, :] < counts[:, None]).reshape(-1)
    two = jnp.arange(2, dtype=jnp.int32)
    table = jnp.stack(
        (
            jnp.concatenate((live.astype(jnp.int32), jnp.ones_like(two))),
            jnp.concatenate((cells, members * capacity + two)),
            jnp.concatenate((order // degree, jnp.full_like(two, slot_key))),
        )
    )
    vmem = pl.BlockSpec(memory_space=pltpu.VMEM)
    smem = pl.BlockSpec(memory_space=pltpu.SMEM)
    hbm = pl.BlockSpec(memory_space=pl.ANY)
    return pl.pallas_call(
        local_kernel,
        out_shape=jax.ShapeDtypeStruct(tokens.shape, tokens.dtype),
        in_specs=[smem, vmem, vmem, vmem, hbm, smem, vmem, vmem],
        out_specs=vmem,
        scratch_shapes=[
            pltpu.VMEM(block.shape, block.dtype),
            pltpu.VMEM((length, 2 * features), jnp.bfloat16),
            pltpu.VMEM(tokens.shape, jnp.float32),
            pltpu.SemaphoreType.DMA,
        ],
        compiler_params=pltpu.CompilerParams(vmem_limit_bytes=60 * 1024 * 1024),
        name="attend_all",
    )(table, queries, w_key, w_value, block, inverse, tokens, w_out)


def sublayer(tokens, w_query, w_key, w_value, w_out, partners, counts, key_slot):
    views = tokens.shape[0]
    members = lax.axis_size("member")
    entries = partners.shape[0] * partners.shape[1]
    capacity = (entries + members - 2) // (members - 1)
    grid = members == LAYERS * ROW and views == capacity + 1
    run = one_kernel if grid else exchange
    return run(tokens, w_query, w_key, w_value, w_out, partners, counts, key_slot[0])


def solution(mesh):
    return jax.shard_map(
        sublayer,
        mesh=mesh,
        in_specs=(
            P(("group", "member"), None, None),
            P(),
            P(),
            P(),
            P(),
            P(("group", "member"), None),
            P(("group", "member")),
            P(("group", "member")),
        ),
        out_specs=P(("group", "member"), None, None),
        check_vma=False,
    )
```

profile of v0, /device:TPU:0, one launch (start us, length us, event | category | flops | bytes accessed | tf_op | source)
XLA Modules:
  0.0 120.3 jit_solution(7940624959628442585)
XLA Ops:
  0.7 0.7 dynamic-slice_bitcast_fusion
  1.4 0.8 reshape.796
  2.1 0.8 reshape.795
  2.9 0.1 pad.5.clone
  3.0 0.1 select_reduce_fusion.4
  3.1 0.2 convert_reduce_fusion
  3.3 0.1 broadcast_compare_fusion.1
  3.4 0.1 broadcast_compare_fusion
  3.4 0.2 and_reduce_fusion
  3.6 0.1 convert_reduce_fusion.1
  3.7 1.2 fusion.7
  4.9 0.7 fusion.1
  5.7 0.6 mul.79.refs_2_
  6.3 0.1 select_reduce_fusion.3
  6.4 0.1 broadcast_add_fusion
  6.5 0.1 select_reduce_fusion.2
  6.7 0.1 select_reduce_fusion.1
  6.8 0.7 reshape.797.refs_1_
  7.5 0.1 select_reduce_fusion
  7.6 0.7 pad_add_fusion.refs_0_
  8.3 2.4 %copy.12.refs_4_ = bf16[4,196,768]{2,1,0:T(8,128)(2,1)} copy(bf16[4,196,768]{2,0,1:T(4,128)(2,1)} %param.9) | data formatting | bytes 2408448 | tf_op args[0]
  10.8 106.7 %sublayer.1 = bf16[4,196,768]{2,1,0:T(8,128)(2,1)} custom-call(s32[5,18]{1,0:T(8,128)} %pad_add_fusion.refs_0_, s32[1,9]{1,0:T(1,128)} %reshape.797.refs_1_, f32[16]{0:T(128)} %mul.79.refs_2_, f32[4]{0:T(128)} %get-tuple-element.5.refs_3_, bf16[4,196,768]{2,1,0:T(8,128)(2,1)} %copy.12.refs_4_, bf16[768,768]{1,0:T(8,128)(2,1)} %refs_5_.1, ...), custom_call_target="tpu_custom_call" | custom-call | tf_op jit(solution)/shard_map/sublayer/pallas_call | solution.py:386
  117.5 2.8 %copy.13 = bf16[4,196,768]{2,0,1:T(4,128)(2,1)} copy(bf16[4,196,768]{2,1,0:T(8,128)(2,1)} %sublayer.1) | data formatting | bytes 2408448 | tf_op jit(solution)/shard_map/sublayer/pallas_call | solution.py:386
  (16 shorter events, 0.1 us)
where the time goes:
time: 121 us; the launch traced here: 120 us
  Pallas kernels  107 us (88%)
  local copies, waits for them, and re-layouts  8.83 us (7%)
  other arithmetic  4 us (3%)
    pallas_call x1, Pallas kernels, one_kernel(): pl.pallas_call(functools.partial(sublayer_kernel, degree, capacity), out_...  107 us
    pallas_call x1, local copies, waits for them, and re-layouts, one_kernel(): pl.pallas_call(functools.partial(sublayer_kernel, degree, capacity), out_...  2.77 us
    unnamed x1, local copies, waits for them, and re-layouts  2.44 us

commit v1 on v0

--- a/solution.py
+++ b/solution.py
@@ -48,11 +48,80 @@
         store(cols, jnp.where(lower, halves[0], halves[1]))
 
 
+RAW_BLOCK, RAW_PLACE, POSITION, BLOCK, PLACE, VIEW = range(6)
+
+
+def build_tables(layer, side, degree, capacity, views, members, partners, key_view, ask, table):
+    entries = views * degree
+    low = layer < LAYERS // 2
+
+    def mirror(value):
+        return jnp.where(low, value, LAYERS - 1 - value)
+
+    here = mirror(layer)
+
+    def read(e, flags):
+        partner = partners[lax.div(e, degree), lax.rem(e, degree)]
+        peer = lax.rem(lax.div(partner, views), members)
+        place = lax.rem(partner, views)
+        there = mirror(lax.div(peer, ROW))
+        inside = jnp.where(there == 0, 1, jnp.where(there == 2, 0, 2))
+        turn = jnp.where(here == 0, there - 1, inside)
+        across = (lax.rem(peer, ROW) != side).astype(jnp.int32)
+        block = jnp.where(there == here, 0, 1 + 2 * turn + across)
+        table[RAW_BLOCK, e] = block
+        table[RAW_PLACE, e] = place
+        return tuple(
+            jnp.where((block == 2 + 2 * (i // views)) & (place == i % views), 1, flag)
+            for i, flag in enumerate(flags)
+        )
+
+    flags = lax.fori_loop(0, entries, read, (jnp.int32(0),) * (3 * views))
+    slots = []
+    for j in range(3):
+        wanted = flags[j * views : (j + 1) * views]
+        slot = capacity - sum(wanted)
+        for v in range(views):
+            slots.append(slot)
+            slot = slot + wanted[v]
+        for k in range(capacity):
+            ask[0, j * capacity + k] = sum(
+                jnp.where((wanted[v] == 1) & (slots[j * views + v] == k), v, 0) for v in range(views)
+            )
+
+    def rank(e, carry):
+        block, place = table[RAW_BLOCK, e], table[RAW_PLACE, e]
+        position = jnp.int32(2)
+        for other in range(entries):
+            ahead = (table[RAW_BLOCK, other] * entries + other) < block * entries + e
+            position = position + ahead.astype(jnp.int32)
+        table[POSITION, e] = position
+        spot = place
+        for i, slot in enumerate(slots):
+            spot = jnp.where((block == 2 + 2 * (i // views)) & (place == i % views), slot, spot)
+        table[RAW_PLACE, e] = spot
+        return carry
+
+    lax.fori_loop(0, entries, rank, 0)
+
+    def sort(r, carry):
+        block, place, view = jnp.int32(-1), jnp.int32(0), key_view
+        for e in range(entries):
+            match = table[POSITION, e] == r
+            block = jnp.where(match, table[RAW_BLOCK, e], block)
+            place = jnp.where(match, table[RAW_PLACE, e], place)
+            view = jnp.where(match, e // degree, view)
+        table[BLOCK, r], table[PLACE, r], table[VIEW, r] = block, place, view
+        return carry
+
+    lax.fori_loop(0, entries + 2, sort, 0)
+
+
 def sublayer_kernel(degree, capacity, *refs):
-    table, ask, weight, key_weight, tokens_in, wq_in, wk_in, wv_in, wo_in, out_ref = refs[:10]
-    tokens, w_query, w_key, w_value, w_out = refs[10:15]
-    own, queries, near, b0, b1, b2, s0, s1, s2, keys, staged, key_out = refs[15:27]
-    asked, cur, pair, results, load_sem, send_sem, recv_sem = refs[27:]
+    partners, counts, key_slot, tokens, wq_in, wk_in, wv_in, wo_in, out_ref = refs[:9]
+    w_query, w_key, w_value, w_out = refs[9:13]
+    own, queries, near, b0, b1, b2, s0, s1, s2, keys, staged, key_out = refs[13:25]
+    ask, asked, table, cur, pair, results, load_sem, send_sem, recv_sem = refs[25:]
     views, length, features = tokens.shape
     members, groups = lax.axis_size("member"), lax.axis_size("group")
     entries = views * degree
@@ -131,7 +200,7 @@
     loads = [
         pltpu.make_async_copy(source, target, load_sem.at[i])
         for i, (source, target) in enumerate(
-            ((tokens_in, tokens), (wq_in, w_query), (wk_in, w_key), (wv_in, w_value), (wo_in, w_out))
+            ((wq_in, w_query), (wk_in, w_key), (wv_in, w_value), (wo_in, w_out))
         )
     ]
     for load in loads:
@@ -145,7 +214,6 @@
     def _():
         pl.semaphore_signal(barrier, inc=1, device_id=outer, device_id_type=MESH)
 
-    loads[0].wait()
     own[0] = layer_norm(tokens[0]).astype(jnp.bfloat16)
 
     @pl.when(is_mid)
@@ -170,15 +238,17 @@
             own_to_b0(v).start()
             own_out(v).start()
 
-    ask_send().start()
-    key_out[...] = own[table[3, 0]]
-    loads[1].wait()
+    key_view = key_slot[0]
+    key_out[...] = own[key_view]
+    loads[0].wait()
     for v in range(views):
         queries[v] = project(own[v], w_query[...]).astype(jnp.bfloat16) * jnp.bfloat16(size**-0.5)
     for i in range(2):
         key_send(i).start()
+    build_tables(layer, side, degree, capacity, views, members, partners, key_view, ask, table)
+    ask_send().start()
+    loads[1].wait()
     loads[2].wait()
-    loads[3].wait()
     for i in range(2):
         key_send(i).wait_recv()
 
@@ -263,7 +333,7 @@
         def _():
             cur[...] = keys[jnp.minimum(t, 1)]
 
-        block, place, view = table[0, t], table[1, t], table[2, t]
+        block, place, view = table[BLOCK, t], table[PLACE, t], table[VIEW, t]
         for j, ref in enumerate(blocks):
             @pl.when(t >= first[j])
             def _():
@@ -278,11 +348,16 @@
 
     ask_send().wait_recv()
     lax.fori_loop(0, entries + 2, entry, 0)
-    loads[4].wait()
+    loads[3].wait()
     for v in range(views):
-        mixed = key_weight[v] * (results[0] + results[1])
+        is_key = (key_view == v).astype(jnp.int32)
+        count = counts[v]
+        mixed = is_key.astype(jnp.float32) * (results[0] + results[1])
         for e in range(degree):
-            mixed += weight[v * degree + e] * results[table[4, v * degree + e]]
+            live = (count > e).astype(jnp.int32).astype(jnp.float32)
+            mixed += live * results[table[POSITION, v * degree + e]]
+        divisor = jnp.full((1, features), count + 2 * is_key, jnp.int32).astype(jnp.float32)
+        mixed = mixed * (1.0 / divisor)
         out_ref[v] = (
             tokens[v].astype(jnp.float32) + project(mixed.astype(jnp.bfloat16), w_out[...])
         ).astype(out_ref.dtype)
@@ -310,73 +385,15 @@
     ask_send().wait_send()
 
 
-def one_kernel(tokens, w_query, w_key, w_value, w_out, partners, counts, slot_key):
+def one_kernel(tokens, w_query, w_key, w_value, w_out, partners, counts, key_slot):
     views, length, features = tokens.shape
     members = lax.axis_size("member")
-    me = lax.axis_index("member")
     degree = partners.shape[1]
-    entry_list = partners.reshape(-1)
-    entries = entry_list.shape[0]
+    entries = views * degree
     capacity = (entries + members - 2) // (members - 1)
-    peers = entry_list // views % members
-    places = entry_list % views
-    layer, side = me // ROW, me % ROW
-    ranking = jnp.array([[9, 0, 1, 2], [1, 9, 0, 2], [2, 0, 9, 1], [2, 1, 0, 9]], jnp.int32)[layer]
-    layers = jnp.arange(LAYERS, dtype=jnp.int32)
-    peer_layer = peers // ROW
-    turn = jnp.sum(jnp.where(peer_layer[:, None] == layers[None, :], ranking[None, :], 0), axis=1)
-    across = peers % ROW != side
-    block = jnp.where(peer_layer == layer, 0, 1 + 2 * turn + across.astype(jnp.int32))
-    order = jnp.arange(entries, dtype=jnp.int32)
-    code = block * entries + order
-    position = jnp.sum((code[None, :] < code[:, None]).astype(jnp.int32), axis=1)
-    spots = jnp.arange(views, dtype=jnp.int32)
-    turns = jnp.arange(LAYERS - 1, dtype=jnp.int32)
-    wanted = jnp.any(
-        (block[None, None, :] == 2 + 2 * turns[:, None, None])
-        & (places[None, None, :] == spots[None, :, None]),
-        axis=2,
-    ).astype(jnp.int32)
-    before = jnp.sum(
-        jnp.where(spots[None, None, :] < spots[None, :, None], wanted[:, None, :], 0), axis=2
-    )
-    slots = capacity - jnp.sum(wanted, axis=1, keepdims=True) + before
-    slot_ids = jnp.arange(capacity, dtype=jnp.int32)
-    ask = jnp.sum(
-        jnp.where(
-            (wanted[:, None, :] == 1) & (slots[:, None, :] == slot_ids[None, :, None]),
-            spots[None, None, :],
-            0,
-        ),
-        axis=2,
-    ).reshape(1, -1)
-    picked = jnp.sum(
-        jnp.where(
-            (block[:, None, None] == 2 + 2 * turns[None, :, None])
-            & (places[:, None, None] == spots[None, None, :]),
-            slots[None, :, :],
-            0,
-        ),
-        axis=(1, 2),
-    )
-    spot = jnp.where((block > 0) & across, picked, places)
-    here = position[None, :] == order[:, None]
-    data = jnp.stack((block, spot, order // degree))
-    data = jnp.sum(jnp.where(here[None], data[:, None, :], 0), axis=2)
-    lead = jnp.stack((jnp.full((2,), -1, jnp.int32), jnp.zeros((2,), jnp.int32), jnp.full((2,), slot_key)))
-    data = jnp.concatenate((lead, data), axis=1)
-    tail = jnp.stack(
-        (jnp.full((entries + 2,), slot_key), jnp.concatenate((position + 2, jnp.zeros((2,), jnp.int32))))
-    )
-    table = jnp.concatenate((data, tail), axis=0)
-    is_key = (spots == slot_key).astype(jnp.int32)
-    inverse = 1.0 / (counts + 2 * is_key).astype(jnp.float32)
-    live = (jnp.arange(degree, dtype=jnp.int32)[None, :] < counts[:, None]).astype(jnp.float32)
-    weight = (live * inverse[:, None]).reshape(-1)
-    key_weight = is_key.astype(jnp.float32) * inverse
-
     smem = pl.BlockSpec(memory_space=pltpu.SMEM)
-    hbm = pl.BlockSpec(memory_space=pl.ANY)
+    hbm = pl.BlockSpec(memory_space=pltpu.HBM)
+    vmem = pl.BlockSpec(memory_space=pltpu.VMEM)
     slab = (length, features)
     weights_shape = pltpu.VMEM((features, features), jnp.bfloat16)
     half = jnp.bfloat16
@@ -386,10 +403,9 @@
     return pl.pallas_call(
         functools.partial(sublayer_kernel, degree, capacity),
         out_shape=jax.ShapeDtypeStruct(tokens.shape, tokens.dtype),
-        in_specs=[smem] * 4 + [hbm] * 5,
-        out_specs=pl.BlockSpec(memory_space=pltpu.VMEM),
+        in_specs=[smem] * 3 + [vmem] + [hbm] * 4,
+        out_specs=vmem,
         scratch_shapes=[
-            pltpu.VMEM(tokens.shape, tokens.dtype),
             weights_shape,
             weights_shape,
             weights_shape,
@@ -398,19 +414,21 @@
             pltpu.VMEM((2, *slab), half),
             pltpu.VMEM((3 * capacity, *slab), half),
             pltpu.VMEM(slab, half),
-            pltpu.SMEM(ask.shape, jnp.int32),
+            pltpu.SMEM((1, 3 * capacity), jnp.int32),
+            pltpu.SMEM((1, 3 * capacity), jnp.int32),
+            pltpu.SMEM((6, entries + 2), jnp.int32),
             pltpu.VMEM(slab, half),
             pltpu.VMEM((length, 2 * features), half),
             pltpu.VMEM((entries + 2, *slab), jnp.float32),
-            pltpu.SemaphoreType.DMA((5,)),
+            pltpu.SemaphoreType.DMA((4,)),
             pltpu.SemaphoreType.DMA((sends,)),
             pltpu.SemaphoreType.DMA((receives,)),
         ],
         compiler_params=pltpu.CompilerParams(
-            collective_id=0, has_side_effects=True, vmem_limit_bytes=60 * 1024 * 1024
+            collective_id=0, has_side_effects=True, vmem_limit_bytes=44 * 1024 * 1024
         ),
         name="sublayer",
-    )(table, ask, weight, key_weight, tokens, w_query, w_key, w_value, w_out)
+    )(partners, counts, key_slot, tokens, w_query, w_key, w_value, w_out)
 
 
 def local_kernel(table, queries, w_key, w_value, block, inverse, tokens, w_out, out_ref, *scratch):
@@ -440,7 +458,8 @@
         out_ref[v] = (tokens[v].astype(jnp.float32) + project(mixed, w_out[...])).astype(out_ref.dtype)
 
 
-def exchange(tokens, w_query, w_key, w_value, w_out, partners, counts, slot_key):
+def exchange(tokens, w_query, w_key, w_value, w_out, partners, counts, key_slot):
+    slot_key = key_slot[0]
     views, length, features = tokens.shape
     members, groups = lax.axis_size("member"), lax.axis_size("group")
     degree = partners.shape[1]
@@ -502,7 +521,7 @@
     capacity = (entries + members - 2) // (members - 1)
     grid = members == LAYERS * ROW and views == capacity + 1
     run = one_kernel if grid else exchange
-    return run(tokens, w_query, w_key, w_value, w_out, partners, counts, key_slot[0])
+    return run(tokens, w_query, w_key, w_value, w_out, partners, counts, key_slot)
 
 
 def solution(mesh):

time: 121 us -> 113 us (0.934)
  other arithmetic: 4 us -> 0 us
  local copies, waits for them, and re-layouts: 8.83 us -> 5.99 us
    reshape x3 -> x0, local copies, waits for them, and re-layouts: 2.19 us -> none  [the longest x2 1.53 us: one_kernel(): entry_list = partners.reshape(-1)]
    unnamed x1 -> x13, local copies, waits for them, and re-layouts: 2.44 us -> 4.5 us
    mul x2 -> x0, other arithmetic: 1.92 us -> none  [the longest x1 1.19 us: one_kernel(): key_weight = is_key.astype(jnp.float32) * inverse]
    pallas_call x1, local copies, waits for them, and re-layouts: 2.77 us -> 1.49 us  [one_kernel(): pl.pallas_call(functools.partial(sublayer_kernel, degree, capacity), out_...]
where the time goes in v1:
time: 113 us
  Pallas kernels  107 us (95%)
  local copies, waits for them, and re-layouts  5.99 us (5%)
    pallas_call x1, Pallas kernels, one_kernel(): pl.pallas_call(functools.partial(sublayer_kernel, degree, capacity), out_...  107 us
    unnamed x13, local copies, waits for them, and re-layouts  4.5 us

profile of v1, /device:TPU:0, one launch (start us, length us, event | category | flops | bytes accessed | tf_op | source)
XLA Modules:
  0.0 113.2 jit_solution(4313870017095504304)
XLA Ops:
  0.7 0.0 copy-start
  0.7 0.0 copy-start.1
  0.7 0.0 copy-start.4
  0.7 0.0 copy-start.5
  0.7 1.6 %copy.9.refs_3_ = bf16[4,196,768]{2,1,0:T(8,128)(2,1)S(1)} copy(bf16[4,196,768]{2,0,1:T(4,128)(2,1)} %param.8) | data formatting | bytes 2408448 | tf_op args[0]
  2.2 0.0 copy-done
  2.3 0.4 copy-done.1
  2.6 0.0 copy-done.4
  2.6 0.0 copy-done.5
  2.6 0.0 copy-start.2
  2.7 1.3 %copy-done.2 = bf16[768,768]{1,0:T(8,128)(2,1)S(1)} copy-done((bf16[768,768]{1,0:T(8,128)(2,1)S(1)}, bf16[768,768]{1,0:T(8,128)(2,1)}, u32[]{:S(2)}) %copy-start.2) | copy-done | bytes 1179672
  3.9 0.0 copy-start.3
  3.9 1.3 %copy-done.3 = bf16[768,768]{1,0:T(8,128)(2,1)S(1)} copy-done((bf16[768,768]{1,0:T(8,128)(2,1)S(1)}, bf16[768,768]{1,0:T(8,128)(2,1)}, u32[]{:S(2)}) %copy-start.3) | copy-done | bytes 1179672
  5.2 106.5 %sublayer.1 = bf16[4,196,768]{2,1,0:T(8,128)(2,1)S(1)} custom-call(s32[4,4]{1,0:T(4,128)S(1)} %copy-done.4, s32[4]{0:T(128)S(1)} %copy-done.5, s32[1]{0:T(128)S(6)} %copy.11.refs_2_, bf16[4,196,768]{2,1,0:T(8,128)(2,1)S(1)} %copy.9.refs_3_, bf16[768,768]{1,0:T(8,128)(2,1)S(1)} %copy-done, bf16[768,768]{1,0:T(8,128)(2,1)S(1)} %copy-done.1, ...), custom_call_target="tpu_custom_call" | custom-call | tf_op jit(solution)/shard_map/sublayer/pallas_call | solution.py:403
  111.7 1.5 %copy.10 = bf16[4,196,768]{2,0,1:T(4,128)(2,1)} copy(bf16[4,196,768]{2,1,0:T(8,128)(2,1)S(1)} %sublayer.1) | data formatting | bytes 2408448 | tf_op jit(solution)/shard_map/sublayer/pallas_call | solution.py:403
Async XLA Ops:
  0.7 1.6 %copy-start = (bf16[768,768]{1,0:T(8,128)(2,1)S(1)}, bf16[768,768]{1,0:T(8,128)(2,1)}, u32[]{:S(2)}) copy-start(bf16[768,768]{1,0:T(8,128)(2,1)} %refs_4_.1) | copy-start | bytes 3538948
  0.7 2.0 %copy-start.1 = (bf16[768,768]{1,0:T(8,128)(2,1)S(1)}, bf16[768,768]{1,0:T(8,128)(2,1)}, u32[]{:S(2)}) copy-start(bf16[768,768]{1,0:T(8,128)(2,1)} %refs_5_.1) | copy-start | bytes 3538948
  0.7 2.0 %copy-start.4 = (s32[4,4]{1,0:T(4,128)S(1)}, s32[4,4]{1,0:T(4,128)}, u32[]{:S(2)}) copy-start(s32[4,4]{1,0:T(4,128)} %refs_0_.1) | copy-start | bytes 196
  0.7 2.0 %copy-start.5 = (s32[4]{0:T(128)S(1)}, s32[4]{0:T(128)}, u32[]{:S(2)}) copy-start(s32[4]{0:T(128)} %refs_1_.1) | copy-start | bytes 52
  2.6 1.3 %copy-start.2 = (bf16[768,768]{1,0:T(8,128)(2,1)S(1)}, bf16[768,768]{1,0:T(8,128)(2,1)}, u32[]{:S(2)}) copy-start(bf16[768,768]{1,0:T(8,128)(2,1)} %refs_6_.1) | copy-start | bytes 3538948
  3.9 1.3 %copy-start.3 = (bf16[768,768]{1,0:T(8,128)(2,1)S(1)}, bf16[768,768]{1,0:T(8,128)(2,1)}, u32[]{:S(2)}) copy-start(bf16[768,768]{1,0:T(8,128)(2,1)} %refs_7_.1) | copy-start | bytes 3538948

commit v2 on v1

--- a/solution.py
+++ b/solution.py
@@ -394,6 +394,9 @@
     smem = pl.BlockSpec(memory_space=pltpu.SMEM)
     hbm = pl.BlockSpec(memory_space=pltpu.HBM)
     vmem = pl.BlockSpec(memory_space=pltpu.VMEM)
+    stay = [
+        pltpu.with_memory_space_constraint(w, pltpu.HBM) for w in (w_query, w_key, w_value, w_out)
+    ]
     slab = (length, features)
     weights_shape = pltpu.VMEM((features, features), jnp.bfloat16)
     half = jnp.bfloat16
@@ -428,7 +431,7 @@
             collective_id=0, has_side_effects=True, vmem_limit_bytes=44 * 1024 * 1024
         ),
         name="sublayer",
-    )(partners, counts, key_slot, tokens, w_query, w_key, w_value, w_out)
+    )(partners, counts, key_slot, tokens, *stay)
 
 
 def local_kernel(table, queries, w_key, w_value, block, inverse, tokens, w_out, out_ref, *scratch):

time: 113 us -> 109 us (0.965)
  local copies, waits for them, and re-layouts: 5.99 us -> 2.91 us
    unnamed x13 -> x5, local copies, waits for them, and re-layouts: 4.5 us -> 1.42 us
where the time goes in v2:
time: 109 us
  Pallas kernels  106 us (97%)
  local copies, waits for them, and re-layouts  2.91 us (3%)
    pallas_call x1, Pallas kernels, one_kernel(): pl.pallas_call(functools.partial(sublayer_kernel, degree, capacity), out_...  106 us

profile of v2, /device:TPU:0, one launch (start us, length us, event | category | flops | bytes accessed | tf_op | source)
XLA Modules:
  0.0 109.1 jit_solution(13493689300979828462)
XLA Ops:
  0.7 0.0 copy-start
  0.7 0.0 copy-start.1
  0.7 1.4 %copy.9.refs_3_ = bf16[4,196,768]{2,1,0:T(8,128)(2,1)S(1)} copy(bf16[4,196,768]{2,0,1:T(4,128)(2,1)} %param.8) | data formatting | bytes 2408448 | tf_op args[0]
  2.1 0.0 copy-done
  2.1 0.0 copy-done.1
  2.1 105.5 %sublayer.1 = bf16[4,196,768]{2,1,0:T(8,128)(2,1)S(1)} custom-call(s32[4,4]{1,0:T(4,128)S(1)} %copy-done, s32[4]{0:T(128)S(1)} %copy-done.1, s32[1]{0:T(128)S(6)} %copy.11.refs_2_, bf16[4,196,768]{2,1,0:T(8,128)(2,1)S(1)} %copy.9.refs_3_, bf16[768,768]{1,0:T(8,128)(2,1)} %refs_4_.1, bf16[768,768]{1,0:T(8,128)(2,1)} %refs_5_.1, bf16[768,768]{1,0:T(8,128)(2,1)} %refs_6_.1, ...), custom_call_target="tpu_custom_call" | custom-call | tf_op jit(solution)/shard_map/sublayer/pallas_call | solution.py:406
  107.6 1.5 %copy.10 = bf16[4,196,768]{2,0,1:T(4,128)(2,1)} copy(bf16[4,196,768]{2,1,0:T(8,128)(2,1)S(1)} %sublayer.1) | data formatting | bytes 2408448 | tf_op jit(solution)/shard_map/sublayer/pallas_call | solution.py:406
Async XLA Ops:
  0.7 1.4 %copy-start = (s32[4,4]{1,0:T(4,128)S(1)}, s32[4,4]{1,0:T(4,128)}, u32[]{:S(2)}) copy-start(s32[4,4]{1,0:T(4,128)} %refs_0_.1) | copy-start | bytes 196
  0.7 1.4 %copy-start.1 = (s32[4]{0:T(128)S(1)}, s32[4]{0:T(128)}, u32[]{:S(2)}) copy-start(s32[4]{0:T(128)} %refs_1_.1) | copy-start | bytes 52

commit v3 on v2

--- a/solution.py
+++ b/solution.py
@@ -432,6 +432,562 @@
         ),
         name="sublayer",
     )(partners, counts, key_slot, tokens, *stay)
+
+
+FAR, WIDE = 9, 7
+FREE, SLOTS, CROSS, PLAIN = 4, 5, 5 + FAR, 5 + FAR + WIDE
+
+
+def quick_kernel(degree, *refs):
+    partners, counts, key_slot, tokens, wq_in, wk_in, wv_in, wo_in, out_ref, flag_ref = refs[:10]
+    w_query, w_key, w_value, w_out = refs[10:14]
+    own, queries, near, b0, b1, b2, first_view, far, wide, keys, far_out, wide_out, key_out = refs[14:27]
+    ask, asked, union, codes, sources, picks, table, cur, pair, results = refs[27:37]
+    load_sem, send_sem, recv_sem = refs[37:40]
+    notes = refs[40:]
+    views, length, features = tokens.shape
+    members, groups = lax.axis_size("member"), lax.axis_size("group")
+    entries = views * degree
+    size = features // HEADS
+    me, group = lax.axis_index("member"), lax.axis_index("group")
+    layer, side = me // ROW, me % ROW
+    low = layer < LAYERS // 2
+    toward = jnp.where(low, ROW, -ROW)
+    is_end = jnp.logical_or(layer == 0, layer == LAYERS - 1)
+    is_mid = jnp.logical_not(is_end)
+    beside = {"member": layer * ROW + 1 - side}
+    inner = {"member": me + toward}
+    outer = {"member": jnp.clip(me - toward, 0, members - 1)}
+    above = {"group": lax.rem(group + 1, groups)}
+    below = {"group": lax.rem(group + groups - 1, groups)}
+    key_view = key_slot[0]
+    cells = 7 * views
+    names = {}
+
+    def number(kind, name):
+        return names.setdefault((kind, name), sum(1 for k, _ in names if k == kind))
+
+    def remote(name, source, target, landing, device):
+        return pltpu.make_async_remote_copy(
+            src_ref=source, dst_ref=target, send_sem=send_sem.at[number(0, name)],
+            recv_sem=recv_sem.at[number(1, landing)], device_id=device, device_id_type=MESH,
+        )
+
+    def to_near(v):
+        return remote(("near", v), own.at[v], near.at[v], ("near", v), beside)
+
+    def own_to_b1(v):
+        return remote(("in", v), own.at[v], b1.at[v], ("b1", v), inner)
+
+    def own_to_b0(v):
+        return remote(("in", v), own.at[v], b0.at[v], ("b0", v), inner)
+
+    def b1_in(v):
+        return remote(("in2", v), b1.at[v], b2.at[v], ("b2", v), inner)
+
+    def own_out():
+        return remote("free", own.at[0], first_view, "free", outer)
+
+    def far_send(q):
+        return remote(("far", q), far_out.at[q], far.at[q], ("far", q), outer)
+
+    def wide_send(k):
+        return remote(("wide", k), wide_out.at[k], wide.at[k], ("wide", k), beside)
+
+    def key_send(i):
+        return remote(("key", i), key_out, keys.at[i], ("key", i), below if i else above)
+
+    def ask_send():
+        return remote("ask", ask, asked, "ask", beside)
+
+    def union_send():
+        return remote("union", union, union, "union", inner)
+
+    def note(i, device):
+        return remote(("note", i), notes[2 * i], notes[2 * i + 1], ("note", i), device)
+
+    loads = [
+        pltpu.make_async_copy(source, target, load_sem.at[i])
+        for i, (source, target) in enumerate(
+            ((wq_in, w_query), (wk_in, w_key), (wv_in, w_value), (wo_in, w_out))
+        )
+    ]
+    for load in loads:
+        load.start()
+    barrier = pltpu.get_barrier_semaphore()
+    for device in (beside, inner, above, below):
+        pl.semaphore_signal(barrier, inc=1, device_id=device, device_id_type=MESH)
+
+    @pl.when(is_mid)
+    def _():
+        pl.semaphore_signal(barrier, inc=1, device_id=outer, device_id_type=MESH)
+
+    def mirror(value):
+        return jnp.where(low, value, LAYERS - 1 - value)
+
+    here = mirror(layer)
+
+    def read(e, carry):
+        partner = partners[lax.div(e, degree), lax.rem(e, degree)]
+        peer = lax.rem(lax.div(partner, views), members)
+        there = mirror(lax.div(peer, ROW))
+        inside = jnp.where(there == 0, 1, jnp.where(there == 2, 0, 2))
+        turn = jnp.where(here == 0, there - 1, inside)
+        across = (lax.rem(peer, ROW) != side).astype(jnp.int32)
+        block = jnp.where(there == here, 0, 1 + 2 * turn + across)
+        live = lax.rem(e, degree) < counts[lax.div(e, degree)]
+        codes[0, e] = jnp.where(live, block * views + lax.rem(partner, views), 0)
+        return carry
+
+    lax.fori_loop(0, entries, read, 0)
+
+    def mark(cell, carry):
+        found = jnp.int32(0)
+        for e in range(entries):
+            found = jnp.where(codes[0, e] == cell, 1, found)
+        ask[0, cell] = found
+        return carry
+
+    lax.fori_loop(0, cells, mark, 0)
+    own[0] = layer_norm(tokens[0]).astype(jnp.bfloat16)
+
+    @pl.when(is_mid)
+    def _():
+        pl.semaphore_wait(barrier, 5)
+
+    @pl.when(is_end)
+    def _():
+        pl.semaphore_wait(barrier, 4)
+
+    ask_send().start()
+    for v in range(views):
+        if v:
+            own[v] = layer_norm(tokens[v]).astype(jnp.bfloat16)
+        to_near(v).start()
+
+        @pl.when(is_end)
+        def _():
+            own_to_b1(v).start()
+
+        @pl.when(is_mid)
+        def _():
+            own_to_b0(v).start()
+            if v == 0:
+                own_out().start()
+
+    key_out[...] = own[key_view]
+    count = 3 * views
+
+    def same(ref, c):
+        return ref[0, (1 + 2 * (c // views)) * views + c % views]
+
+    def cross(ref, c):
+        return ref[0, (2 + 2 * (c // views)) * views + c % views]
+
+    ask_send().wait_recv()
+
+    @pl.when(is_end)
+    def _():
+        for c in range(count):
+            union[0, c] = jnp.maximum(same(ask, c), cross(asked, c))
+        union_send().start()
+
+    loads[0].wait()
+    for v in range(views):
+        queries[v] = project(own[v], w_query[...]).astype(jnp.bfloat16) * jnp.bfloat16(size**-0.5)
+    for i in range(2):
+        key_send(i).start()
+
+    @pl.when(is_mid)
+    def _():
+        union_send().wait_recv()
+
+    def line_up(flags, ready):
+        spots, last = [], jnp.int32(-1)
+        for flag, at in zip(flags, ready):
+            spot = jnp.maximum(last + 1, at)
+            spots.append(spot)
+            last = jnp.where(flag == 1, spot, last)
+        return spots, last
+
+    far_ready = [0] * views + [v + 1 for v in range(views)] + [v + 1 + views for v in range(views)]
+
+    def far_slots(flags):
+        spots, last = line_up(flags[1:], far_ready[1:])
+        return [jnp.int32(-1)] + spots, last
+
+    def wide_slots(flags, behind):
+        ready = []
+        for c in range(count):
+            late = 0 if c < 2 * views else c - 2 * views + 1
+            ready.append(jnp.where(is_end, jnp.maximum(behind[c] - 2, 0), late))
+        return line_up(flags, ready)
+
+    def found(c, spots):
+        return jnp.where(is_end, FREE if c == 0 else SLOTS + spots[c], PLAIN + c)
+
+    mine = [union[0, c] for c in range(count)]
+    my_far, far_last = far_slots(mine)
+    beside_far, _ = far_slots([jnp.maximum(same(asked, c), cross(ask, c)) for c in range(count)])
+    out_flags = [cross(asked, c) for c in range(count)]
+    my_wide, out_last = wide_slots(out_flags, my_far)
+    beside_wide, in_last = wide_slots([cross(ask, c) for c in range(count)], beside_far)
+    for q in range(FAR):
+        pick = jnp.int32(0)
+        for c in range(1, count):
+            pick = jnp.where((mine[c] == 1) & (my_far[c] == q), c, pick)
+        picks[0, q] = pick
+    for k in range(WIDE):
+        pick = jnp.where(is_end, FREE, PLAIN)
+        for c in range(count):
+            pick = jnp.where((out_flags[c] == 1) & (my_wide[c] == k), found(c, my_far), pick)
+        picks[0, FAR + k] = pick
+    for v in range(views):
+        sources[0, v] = v
+    for c in range(count):
+        sources[0, (1 + 2 * (c // views)) * views + c % views] = found(c, my_far)
+        sources[0, (2 + 2 * (c // views)) * views + c % views] = CROSS + beside_wide[c]
+    full = (far_last >= FAR) | (out_last >= WIDE) | (in_last >= WIDE)
+    notes[0][0, 0] = full.astype(jnp.int32)
+
+    def choose(choice, options):
+        value = None
+        for key, load in options:
+            value = load() if value is None else jnp.where(choice == key, load(), value)
+        return value
+
+    def far_stage(q):
+        options = [(c, functools.partial(own.__getitem__, c)) for c in range(min(views, q + views))]
+        options += [(views + v, functools.partial(b0.__getitem__, v)) for v in range(views) if v < q]
+        options += [
+            (2 * views + v, functools.partial(b2.__getitem__, v)) for v in range(views) if v + views < q
+        ]
+        far_out[q] = choose(picks[0, q], options)
+        far_send(q).start()
+
+    def far_turn(q):
+        @pl.when(is_mid)
+        def _():
+            if 1 <= q <= views:
+                own_to_b0(q - 1).wait_recv()
+                own_to_b1(q - 1).wait_recv()
+                b1_in(q - 1).start()
+            if q > views:
+                b1_in(q - 1 - views).wait_recv()
+            far_stage(q)
+
+    def wide_stage(k):
+        choice = picks[0, FAR + k]
+
+        @pl.when(is_end)
+        def _():
+            options = [(FREE, lambda: first_view[...])]
+            options += [(SLOTS + q, functools.partial(far.__getitem__, q)) for q in range(k + 3)]
+            wide_out[k] = choose(choice, options)
+
+        @pl.when(is_mid)
+        def _():
+            options = [(PLAIN + v, functools.partial(b0.__getitem__, v)) for v in range(views)]
+            options += [(PLAIN + views + v, functools.partial(b1.__getitem__, v)) for v in range(views)]
+            options += [
+                (PLAIN + 2 * views + v, functools.partial(b2.__getitem__, v))
+                for v in range(views)
+                if v < k
+            ]
+            wide_out[k] = choose(choice, options)
+
+        wide_send(k).start()
+
+    def far_arrive(q):
+        @pl.when(is_end)
+        def _():
+            far_send(q).wait_recv()
+
+    def wide_turn(k):
+        far_arrive(k + 2)
+        wide_stage(k)
+
+    def note_value(i, value):
+        notes[2 * i][0, 0] = value
+
+    def seen(i):
+        return notes[2 * i + 1][0, 0]
+
+    rounds = groups // 2
+
+    def note_step(i):
+        if i == 0:
+            note(0, beside).start()
+        if i == 1:
+            note(0, beside).wait_recv()
+            note_value(1, jnp.maximum(notes[0][0, 0], seen(0)))
+
+            @pl.when(is_end)
+            def _():
+                note(1, inner).start()
+        if i == 2:
+            @pl.when(is_mid)
+            def _():
+                note(1, inner).wait_recv()
+                note_value(2, jnp.maximum(notes[2][0, 0], seen(1)))
+                note(2, inner).start()
+        if i == 3:
+            @pl.when(is_mid)
+            def _():
+                note(2, inner).wait_recv()
+                note_value(3, jnp.maximum(notes[4][0, 0], seen(2)))
+                note(3, outer).start()
+                note_value(4, notes[6][0, 0])
+        if i == 4:
+            @pl.when(is_end)
+            def _():
+                note(3, outer).wait_recv()
+                note_value(4, seen(3))
+
+            note_value(5, notes[8][0, 0])
+            note(4, above).start()
+            note(5, below).start()
+        if i > 4:
+            j = 2 * i - 6
+            note(j, above).wait_recv()
+            note(j + 1, below).wait_recv()
+            value = jnp.maximum(notes[2 * j][0, 0], jnp.maximum(seen(j), seen(j + 1)))
+            if i < 4 + rounds:
+                note_value(j + 2, value)
+                note_value(j + 3, value)
+                note(j + 2, above).start()
+                note(j + 3, below).start()
+            else:
+                flag_ref[0, 0] = value
+
+    far_turn(0)
+    note_step(0)
+
+    def rank(e, carry):
+        code = codes[0, e] * entries + e
+        position = jnp.int32(2)
+        for other in range(entries):
+            position = position + (codes[0, other] * entries + other < code).astype(jnp.int32)
+        table[0, e] = position
+        return carry
+
+    lax.fori_loop(0, entries, rank, 0)
+
+    def sort(r, carry):
+        cell, view = jnp.int32(0), key_view
+        for e in range(entries):
+            match = table[0, e] == r
+            cell = jnp.where(match, codes[0, e], cell)
+            view = jnp.where(match, e // degree, view)
+        table[1, r], table[2, r] = sources[0, cell], view
+        return carry
+
+    lax.fori_loop(0, entries + 2, sort, 0)
+    loads[1].wait()
+    loads[2].wait()
+    for i in range(2):
+        key_send(i).wait_recv()
+
+    late = [2 + max(0, entries - n) for n in (15, 12, 9, 7, 3)]
+    turns = {
+        1: [lambda: far_turn(1), lambda: note_step(1)],
+        2: [lambda: far_turn(2), lambda: far_turn(3), lambda: far_turn(4)]
+        + [functools.partial(far_arrive, q) for q in range(2)],
+        late[0]: [lambda: far_turn(5), lambda: wide_turn(1), lambda: far_turn(6)]
+        + [lambda: wide_turn(2), lambda: note_step(3)],
+        late[1]: [lambda: far_turn(8), lambda: wide_turn(4), lambda: note_step(4)],
+        late[2]: [lambda: wide_turn(5), lambda: note_step(5)],
+        late[3]: [lambda: wide_turn(6), lambda: note_step(6)],
+        late[4]: [],
+    }
+
+    def events(t):
+        for turn in turns[t]:
+            turn()
+        if t == 2:
+            @pl.when(is_end)
+            def _():
+                own_out().wait_recv()
+
+            for v in range(views):
+                to_near(v).wait_recv()
+            wide_turn(0)
+            note_step(2)
+        if t == late[0]:
+            for k in range(3):
+                wide_send(k).wait_recv()
+            far_turn(7)
+            wide_turn(3)
+        if t == late[2]:
+            wide_send(3).wait_recv()
+            wide_send(4).wait_recv()
+        if t == late[3]:
+            wide_send(5).wait_recv()
+        if t == late[4]:
+            wide_send(6).wait_recv()
+
+    def entry(t, carry):
+        for when in turns:
+            @pl.when(t == when)
+            def _():
+                events(when)
+
+        source, view = table[1, t], table[2, t]
+
+        def take(condition, key, load):
+            @pl.when(condition)
+            def _():
+                cur[...] = jnp.where(source == key, load(), cur[...])
+
+        def take_any(condition, start, ref):
+            spot = source - start
+            held = ref.shape[0]
+
+            @pl.when(condition)
+            def _():
+                value = ref[jnp.clip(spot, 0, held - 1)]
+                cur[...] = jnp.where((spot >= 0) & (spot < held), value, cur[...])
+
+        @pl.when(t < 2)
+        def _():
+            cur[...] = keys[jnp.minimum(t, 1)]
+
+        take_any(t >= 2, 0, near)
+        for j, ref in enumerate((b0, b1)):
+            take_any((t >= 2) & is_mid, PLAIN + j * views, ref)
+        take_any((t >= late[1]) & is_mid, PLAIN + 2 * views, b2)
+        take((t >= 2) & is_end, FREE, lambda: first_view[...])
+        for q in range(FAR - 2):
+            since = 2 if q < 3 else late[1]
+            take(
+                (t >= since) & (t < late[3]) & is_end, SLOTS + q,
+                functools.partial(far.__getitem__, q),
+            )
+        take_any((t >= late[3]) & is_end, SLOTS, far)
+        for k in range(WIDE - 1):
+            since = late[0] if k < 3 else (late[2] if k < 5 else late[3])
+            take((t >= since) & (t < late[4]), CROSS + k, functools.partial(wide.__getitem__, k))
+        take_any(t >= late[4], CROSS, wide)
+
+        def store(cols, value):
+            results[t, :, cols] = value
+
+        attend(lambda cols: queries[view, :, cols], cur[...], w_key, w_value, pair, store)
+        return carry
+
+    lax.fori_loop(0, entries + 2, entry, 0)
+    loads[3].wait()
+    for v in range(views):
+        is_key = (key_view == v).astype(jnp.int32)
+        total = counts[v]
+        mixed = is_key.astype(jnp.float32) * (results[0] + results[1])
+        for e in range(degree):
+            live = (total > e).astype(jnp.int32).astype(jnp.float32)
+            mixed += live * results[table[0, v * degree + e]]
+        divisor = jnp.full((1, features), total + 2 * is_key, jnp.int32).astype(jnp.float32)
+        mixed = mixed * (1.0 / divisor)
+        out_ref[v] = (
+            tokens[v].astype(jnp.float32) + project(mixed.astype(jnp.bfloat16), w_out[...])
+        ).astype(out_ref.dtype)
+
+    for v in range(views):
+        to_near(v).wait_send()
+
+        @pl.when(is_end)
+        def _():
+            own_to_b1(v).wait_send()
+
+        @pl.when(is_mid)
+        def _():
+            own_to_b0(v).wait_send()
+            b1_in(v).wait_send()
+
+    @pl.when(is_mid)
+    def _():
+        own_out().wait_send()
+        for q in range(FAR):
+            far_send(q).wait_send()
+        note(2, inner).wait_send()
+        note(3, outer).wait_send()
+
+    @pl.when(is_end)
+    def _():
+        union_send().wait_send()
+        note(1, inner).wait_send()
+
+    for k in range(WIDE):
+        wide_send(k).wait_send()
+    for i in range(2):
+        key_send(i).wait_send()
+    ask_send().wait_send()
+    note(0, beside).wait_send()
+    for i in range(4, 4 + 2 * rounds):
+        note(i, above if i % 2 == 0 else below).wait_send()
+
+
+def quick(tokens, w_query, w_key, w_value, w_out, partners, counts, key_slot):
+    views, length, features = tokens.shape
+    degree = partners.shape[1]
+    entries = views * degree
+    rounds = lax.axis_size("group") // 2
+    smem = pl.BlockSpec(memory_space=pltpu.SMEM)
+    hbm = pl.BlockSpec(memory_space=pltpu.HBM)
+    vmem = pl.BlockSpec(memory_space=pltpu.VMEM)
+    stay = [
+        pltpu.with_memory_space_constraint(w, pltpu.HBM) for w in (w_query, w_key, w_value, w_out)
+    ]
+    slab = (length, features)
+    half = jnp.bfloat16
+
+    def slabs(count):
+        return pltpu.VMEM((count, *slab), half)
+
+    def numbers(*shape):
+        return pltpu.SMEM(shape, jnp.int32)
+
+    return pl.pallas_call(
+        functools.partial(quick_kernel, degree),
+        out_shape=(
+            jax.ShapeDtypeStruct(tokens.shape, tokens.dtype),
+            jax.ShapeDtypeStruct((1, 1), jnp.int32),
+        ),
+        in_specs=[smem] * 3 + [vmem] + [hbm] * 4,
+        out_specs=(vmem, smem),
+        scratch_shapes=[
+            *[pltpu.VMEM((features, features), half)] * 4,
+            *[slabs(views)] * 6,
+            pltpu.VMEM(slab, half),
+            slabs(FAR),
+            slabs(WIDE),
+            slabs(2),
+            slabs(FAR),
+            slabs(WIDE),
+            pltpu.VMEM(slab, half),
+            numbers(1, 7 * views),
+            numbers(1, 7 * views),
+            numbers(1, 3 * views),
+            numbers(1, entries),
+            numbers(1, 7 * views),
+            numbers(1, FAR + WIDE),
+            numbers(3, entries + 2),
+            pltpu.VMEM(slab, half),
+            pltpu.VMEM((length, 2 * features), half),
+            pltpu.VMEM((entries + 2, *slab), jnp.float32),
+            pltpu.SemaphoreType.DMA((4,)),
+            pltpu.SemaphoreType.DMA((5 * views + FAR + WIDE + 16,)),
+            pltpu.SemaphoreType.DMA((5 * views + FAR + WIDE + 16,)),
+            *[numbers(1, 1)] * (2 * (4 + 2 * rounds)),
+        ],
+        compiler_params=pltpu.CompilerParams(
+            collective_id=1, has_side_effects=True, vmem_limit_bytes=48 * 1024 * 1024
+        ),
+        name="sublayer_quick",
+    )(partners, counts, key_slot, tokens, *stay)
+
+
+def select_kernel(*arguments):
+    result, flag = quick(*arguments)
+    return lax.cond(flag[0, 0] > 0, lambda: one_kernel(*arguments), lambda: result)
 
 
 def local_kernel(table, queries, w_key, w_value, block, inverse, tokens, w_out, out_ref, *scratch):
@@ -523,7 +1079,7 @@
     entries = partners.shape[0] * partners.shape[1]
     capacity = (entries + members - 2) // (members - 1)
     grid = members == LAYERS * ROW and views == capacity + 1
-    run = one_kernel if grid else exchange
+    run = select_kernel if grid else exchange
     return run(tokens, w_query, w_key, w_value, w_out, partners, counts, key_slot)
 
 

time: 109 us -> 117 us (1.073)
  Pallas kernels: 106 us -> 112 us
    pallas_call x1, Pallas kernels: 106 us -> 112 us  [quick(): pl.pallas_call(functools.partial(quick_kernel, degree), out_shape=(jax.Sh...]
    unnamed x5 -> x8, local copies, waits for them, and re-layouts: 1.42 us -> 2.92 us
    pallas_call x1 -> x0, local copies, waits for them, and re-layouts: 1.49 us -> none  [one_kernel(): pl.pallas_call(functools.partial(sublayer_kernel, degree, capacity), out_...]
where the time goes in v3:
time: 117 us; the launch traced here: 116 us
  Pallas kernels  112 us (96%)
  local copies, waits for them, and re-layouts  2.92 us (2%)
  between operations  1.28 us (1%)
    pallas_call x1, Pallas kernels, quick(): pl.pallas_call(functools.partial(quick_kernel, degree), out_shape=(jax.Sh...  112 us
    unnamed x8, local copies, waits for them, and re-layouts  2.92 us

profile of v3, /device:TPU:0, one launch (start us, length us, event | category | flops | bytes accessed | tf_op | source)
XLA Modules:
  0.0 116.1 jit_solution(16541075944139407730)
XLA Ops:
  0.7 0.0 copy-start.1
  0.7 0.0 copy-start.2
  0.7 1.4 %copy.11.refs_3_ = bf16[4,196,768]{2,1,0:T(8,128)(2,1)S(1)} copy(bf16[4,196,768]{2,0,1:T(4,128)(2,1)} %param.10) | data formatting | bytes 2408448 | tf_op args[0]
  2.1 0.0 copy-done.1
  2.1 0.0 copy-done.2
  2.1 0.0 copy-start
  2.1 111.6 %sublayer_quick.1 = (bf16[4,196,768]{2,1,0:T(8,128)(2,1)S(1)}, s32[1,1]{1,0:T(1,128)}) custom-call(s32[4,4]{1,0:T(4,128)S(1)} %copy-done.1, s32[4]{0:T(128)S(1)} %copy-done.2, s32[1]{0:T(128)S(6)} %copy.16.refs_2_, bf16[4,196,768]{2,1,0:T(8,128)(2,1)S(1)} %copy.11.refs_3_, bf16[768,768]{1,0:T(8,128)(2,1)} %refs_4_.1, bf16[768,768]{1,0:T(8,128)(2,1)} %refs_5_.1, ...), custom_call_target="tpu_custom_call" | custom-call | tf_op jit(solution)/shard_map/sublayer_quick/pallas_call | solution.py:948
  114.3 0.0 copy-done
  114.3 0.2 conditional.1
  114.6 1.5 %copy.13 = bf16[4,196,768]{2,0,1:T(4,128)(2,1)} copy(bf16[4,196,768]{2,1,0:T(8,128)(2,1)S(1)} %get-tuple-element.37) | data formatting | bytes 2408448
Async XLA Ops:
  0.7 1.4 %copy-start.1 = (s32[4,4]{1,0:T(4,128)S(1)}, s32[4,4]{1,0:T(4,128)}, u32[]{:S(2)}) copy-start(s32[4,4]{1,0:T(4,128)} %refs_0_.1) | copy-start | bytes 196
  0.7 1.4 %copy-start.2 = (s32[4]{0:T(128)S(1)}, s32[4]{0:T(128)}, u32[]{:S(2)}) copy-start(s32[4]{0:T(128)} %refs_1_.1) | copy-start | bytes 52
  2.1 112.2 %copy-start = (bf16[4,196,768]{2,0,1:T(4,128)(2,1)S(1)}, bf16[4,196,768]{2,0,1:T(4,128)(2,1)}, u32[]{:S(2)}) copy-start(bf16[4,196,768]{2,0,1:T(4,128)(2,1)} %param.10) | copy-start | bytes 3612676

commit v4 on v3

--- a/solution.py
+++ b/solution.py
@@ -565,10 +565,6 @@
             own[v] = layer_norm(tokens[v]).astype(jnp.bfloat16)
         to_near(v).start()
 
-        @pl.when(is_end)
-        def _():
-            own_to_b1(v).start()
-
         @pl.when(is_mid)
         def _():
             own_to_b0(v).start()
@@ -591,6 +587,8 @@
         for c in range(count):
             union[0, c] = jnp.maximum(same(ask, c), cross(asked, c))
         union_send().start()
+        for v in range(views):
+            own_to_b1(v).start()
 
     loads[0].wait()
     for v in range(views):
@@ -670,11 +668,12 @@
         def _():
             if 1 <= q <= views:
                 own_to_b0(q - 1).wait_recv()
-                own_to_b1(q - 1).wait_recv()
-                b1_in(q - 1).start()
             if q > views:
                 b1_in(q - 1 - views).wait_recv()
             far_stage(q)
+            if 1 <= q <= views:
+                own_to_b1(q - 1).wait_recv()
+                b1_in(q - 1).start()
 
     def wide_stage(k):
         choice = picks[0, FAR + k]
@@ -790,16 +789,18 @@
 
     late = [2 + max(0, entries - n) for n in (15, 12, 9, 7, 3)]
     turns = {
-        1: [lambda: far_turn(1), lambda: note_step(1)],
+        1: [lambda: far_turn(1)],
         2: [lambda: far_turn(2), lambda: far_turn(3), lambda: far_turn(4)]
         + [functools.partial(far_arrive, q) for q in range(2)],
         late[0]: [lambda: far_turn(5), lambda: wide_turn(1), lambda: far_turn(6)]
-        + [lambda: wide_turn(2), lambda: note_step(3)],
-        late[1]: [lambda: far_turn(8), lambda: wide_turn(4), lambda: note_step(4)],
-        late[2]: [lambda: wide_turn(5), lambda: note_step(5)],
-        late[3]: [lambda: wide_turn(6), lambda: note_step(6)],
+        + [lambda: wide_turn(2)],
+        late[1]: [lambda: far_turn(8), lambda: wide_turn(4), lambda: note_step(3)],
+        late[2]: [lambda: wide_turn(5)],
+        late[3]: [lambda: wide_turn(6)],
         late[4]: [],
     }
+    for i in range(1, rounds + 1):
+        turns[late[3] + i] = [functools.partial(note_step, 4 + i)]
 
     def events(t):
         for turn in turns[t]:
@@ -812,17 +813,19 @@
             for v in range(views):
                 to_near(v).wait_recv()
             wide_turn(0)
-            note_step(2)
+            note_step(1)
         if t == late[0]:
             for k in range(3):
                 wide_send(k).wait_recv()
             far_turn(7)
             wide_turn(3)
+            note_step(2)
         if t == late[2]:
             wide_send(3).wait_recv()
             wide_send(4).wait_recv()
         if t == late[3]:
             wide_send(5).wait_recv()
+            note_step(4)
         if t == late[4]:
             wide_send(6).wait_recv()
 

time: 117 us -> 98.6 us (0.84)
  Pallas kernels: 112 us -> 94 us
    pallas_call x1, Pallas kernels: 112 us -> 94 us  [quick(): pl.pallas_call(functools.partial(quick_kernel, degree), out_shape=(jax.Sh...]
where the time goes in v4:
time: 98.6 us; the launch traced here: 98.4 us
  Pallas kernels  94 us (95%)
  local copies, waits for them, and re-layouts  2.92 us (3%)
  between operations  1.28 us (1%)
    pallas_call x1, Pallas kernels, quick(): pl.pallas_call(functools.partial(quick_kernel, degree), out_shape=(jax.Sh...  94 us
    unnamed x8, local copies, waits for them, and re-layouts  2.92 us

profile of v4, /device:TPU:0, one launch (start us, length us, event | category | flops | bytes accessed | tf_op | source)
XLA Modules:
  0.0 98.4 jit_solution(16920067952290553288)
XLA Ops:
  0.7 0.0 copy-start.1
  0.7 0.0 copy-start.2
  0.7 1.4 %copy.11.refs_3_ = bf16[4,196,768]{2,1,0:T(8,128)(2,1)S(1)} copy(bf16[4,196,768]{2,0,1:T(4,128)(2,1)} %param.10) | data formatting | bytes 2408448 | tf_op args[0]
  2.1 0.0 copy-done.1
  2.1 0.0 copy-done.2
  2.1 0.0 copy-start
  2.1 94.0 %sublayer_quick.1 = (bf16[4,196,768]{2,1,0:T(8,128)(2,1)S(1)}, s32[1,1]{1,0:T(1,128)}) custom-call(s32[4,4]{1,0:T(4,128)S(1)} %copy-done.1, s32[4]{0:T(128)S(1)} %copy-done.2, s32[1]{0:T(128)S(6)} %copy.16.refs_2_, bf16[4,196,768]{2,1,0:T(8,128)(2,1)S(1)} %copy.11.refs_3_, bf16[768,768]{1,0:T(8,128)(2,1)} %refs_4_.1, bf16[768,768]{1,0:T(8,128)(2,1)} %refs_5_.1, ...), custom_call_target="tpu_custom_call" | custom-call | tf_op jit(solution)/shard_map/sublayer_quick/pallas_call | solution.py:951
  96.7 0.0 copy-done
  96.7 0.2 conditional.1
  96.9 1.5 %copy.13 = bf16[4,196,768]{2,0,1:T(4,128)(2,1)} copy(bf16[4,196,768]{2,1,0:T(8,128)(2,1)S(1)} %get-tuple-element.37) | data formatting | bytes 2408448
Async XLA Ops:
  0.7 1.4 %copy-start.1 = (s32[4,4]{1,0:T(4,128)S(1)}, s32[4,4]{1,0:T(4,128)}, u32[]{:S(2)}) copy-start(s32[4,4]{1,0:T(4,128)} %refs_0_.1) | copy-start | bytes 196
  0.7 1.4 %copy-start.2 = (s32[4]{0:T(128)S(1)}, s32[4]{0:T(128)}, u32[]{:S(2)}) copy-start(s32[4]{0:T(128)} %refs_1_.1) | copy-start | bytes 52
  2.1 94.6 %copy-start = (bf16[4,196,768]{2,0,1:T(4,128)(2,1)S(1)}, bf16[4,196,768]{2,0,1:T(4,128)(2,1)}, u32[]{:S(2)}) copy-start(bf16[4,196,768]{2,0,1:T(4,128)(2,1)} %param.10) | copy-start | bytes 3612676

commit v5 on v4

--- a/solution.py
+++ b/solution.py
@@ -26,10 +26,14 @@
 
 def attend(query, normed, w_key, w_value, pair, store):
     features = normed.shape[1]
+    pair[:, :features] = project(normed, w_key[...]).astype(jnp.bfloat16)
+    pair[:, features:] = project(normed, w_value[...]).astype(jnp.bfloat16)
+    heads(query, pair, features, store)
+
+
+def heads(query, pair, features, store):
     size = features // HEADS
     lower = lax.broadcasted_iota(jnp.int32, (1, 2 * size), 1) < size
-    pair[:, :features] = project(normed, w_key[...]).astype(jnp.bfloat16)
-    pair[:, features:] = project(normed, w_value[...]).astype(jnp.bfloat16)
     for h in range(HEADS // 2):
         cols = pl.ds(2 * h * size, 2 * size)
         rows = query(cols)
@@ -435,16 +439,17 @@
 
 
 FAR, WIDE = 9, 7
-FREE, SLOTS, CROSS, PLAIN = 4, 5, 5 + FAR, 5 + FAR + WIDE
+FREE, SLOTS, PLAIN, CROSS = 4, 5, 4, 16
+KEYS = CROSS + WIDE
 
 
 def quick_kernel(degree, *refs):
     partners, counts, key_slot, tokens, wq_in, wk_in, wv_in, wo_in, out_ref, flag_ref = refs[:10]
     w_query, w_key, w_value, w_out = refs[10:14]
-    own, queries, near, b0, b1, b2, first_view, far, wide, keys, far_out, wide_out, key_out = refs[14:27]
-    ask, asked, union, codes, sources, picks, table, cur, pair, results = refs[27:37]
-    load_sem, send_sem, recv_sem = refs[37:40]
-    notes = refs[40:]
+    own, queries, near, landing, wide, keys, far_out, wide_out, key_out = refs[14:23]
+    ask, asked, union, codes, sources, picks, table, pairs, results = refs[23:32]
+    load_sem, send_sem, recv_sem = refs[32:35]
+    notes = refs[35:]
     views, length, features = tokens.shape
     members, groups = lax.axis_size("member"), lax.axis_size("group")
     entries = views * degree
@@ -462,6 +467,8 @@
     below = {"group": lax.rem(group + groups - 1, groups)}
     key_view = key_slot[0]
     cells = 7 * views
+    b0, b1, b2 = (landing.at[pl.ds(i * views, views)] for i in range(3))
+    first_view, far = landing.at[pl.ds(0, 1)], landing.at[pl.ds(1, FAR)]
     names = {}
 
     def number(kind, name):
@@ -486,7 +493,7 @@
         return remote(("in2", v), b1.at[v], b2.at[v], ("b2", v), inner)
 
     def own_out():
-        return remote("free", own.at[0], first_view, "free", outer)
+        return remote("free", own.at[0], first_view.at[0], "free", outer)
 
     def far_send(q):
         return remote(("far", q), far_out.at[q], far.at[q], ("far", q), outer)
@@ -648,6 +655,9 @@
     full = (far_last >= FAR) | (out_last >= WIDE) | (in_last >= WIDE)
     notes[0][0, 0] = full.astype(jnp.int32)
 
+    def view_of(ref, index):
+        return ref[index]
+
     def choose(choice, options):
         value = None
         for key, load in options:
@@ -655,10 +665,10 @@
         return value
 
     def far_stage(q):
-        options = [(c, functools.partial(own.__getitem__, c)) for c in range(min(views, q + views))]
-        options += [(views + v, functools.partial(b0.__getitem__, v)) for v in range(views) if v < q]
+        options = [(c, functools.partial(view_of, own, c)) for c in range(min(views, q + views))]
+        options += [(views + v, functools.partial(view_of, b0, v)) for v in range(views) if v < q]
         options += [
-            (2 * views + v, functools.partial(b2.__getitem__, v)) for v in range(views) if v + views < q
+            (2 * views + v, functools.partial(view_of, b2, v)) for v in range(views) if v + views < q
         ]
         far_out[q] = choose(picks[0, q], options)
         far_send(q).start()
@@ -680,16 +690,16 @@
 
         @pl.when(is_end)
         def _():
-            options = [(FREE, lambda: first_view[...])]
-            options += [(SLOTS + q, functools.partial(far.__getitem__, q)) for q in range(k + 3)]
+            options = [(FREE, lambda: first_view[0])]
+            options += [(SLOTS + q, functools.partial(view_of, far, q)) for q in range(k + 3)]
             wide_out[k] = choose(choice, options)
 
         @pl.when(is_mid)
         def _():
-            options = [(PLAIN + v, functools.partial(b0.__getitem__, v)) for v in range(views)]
-            options += [(PLAIN + views + v, functools.partial(b1.__getitem__, v)) for v in range(views)]
+            options = [(PLAIN + v, functools.partial(view_of, b0, v)) for v in range(views)]
+            options += [(PLAIN + views + v, functools.partial(view_of, b1, v)) for v in range(views)]
             options += [
-                (PLAIN + 2 * views + v, functools.partial(b2.__getitem__, v))
+                (PLAIN + 2 * views + v, functools.partial(view_of, b2, v))
                 for v in range(views)
                 if v < k
             ]
@@ -778,7 +788,7 @@
             match = table[0, e] == r
             cell = jnp.where(match, codes[0, e], cell)
             view = jnp.where(match, e // degree, view)
-        table[1, r], table[2, r] = sources[0, cell], view
+        table[1, r], table[2, r] = jnp.where(r < 2, KEYS + r, sources[0, cell]), view
         return carry
 
     lax.fori_loop(0, entries + 2, sort, 0)
@@ -786,6 +796,27 @@
     loads[2].wait()
     for i in range(2):
         key_send(i).wait_recv()
+
+    def learn(place, ref, start, count):
+        def one(i, carry):
+            rows = ref[start + i]
+            pairs[place + i, :, :features] = project(rows, w_key[...]).astype(jnp.bfloat16)
+            pairs[place + i, :, features:] = project(rows, w_value[...]).astype(jnp.bfloat16)
+            return carry
+
+        lax.fori_loop(0, count, one, 0)
+
+    def learn_far(first, last):
+        @pl.when(is_end)
+        def _():
+            learn(SLOTS + first, far, first, last - first)
+
+    def learn_last(first, last):
+        @pl.when(is_mid)
+        def _():
+            learn(PLAIN + 2 * views + first, b2, first, last - first)
+
+    learn(KEYS, keys, 0, 2)
 
     late = [2 + max(0, entries - n) for n in (15, 12, 9, 7, 3)]
     turns = {
@@ -814,20 +845,45 @@
                 to_near(v).wait_recv()
             wide_turn(0)
             note_step(1)
+            learn(0, near, 0, views)
+
+            @pl.when(is_end)
+            def _():
+                learn(FREE, first_view, 0, 1)
+
+            @pl.when(is_mid)
+            def _():
+                learn(PLAIN, b0, 0, views)
+                learn(PLAIN + views, b1, 0, views)
+
+            learn_far(0, 3)
         if t == late[0]:
+            learn_far(3, 5)
+            learn_last(0, 2)
             for k in range(3):
                 wide_send(k).wait_recv()
             far_turn(7)
             wide_turn(3)
             note_step(2)
+            learn(CROSS, wide, 0, 3)
+            learn_far(5, 6)
+            learn_last(2, 3)
+        if t == late[1]:
+            learn_far(6, 7)
+            learn_last(3, 4)
         if t == late[2]:
             wide_send(3).wait_recv()
             wide_send(4).wait_recv()
+            learn(CROSS + 3, wide, 3, 2)
+            learn_far(7, 8)
         if t == late[3]:
             wide_send(5).wait_recv()
             note_step(4)
+            learn(CROSS + 5, wide, 5, 1)
+            learn_far(8, 9)
         if t == late[4]:
             wide_send(6).wait_recv()
+            learn(CROSS + 6, wide, 6, 1)
 
     def entry(t, carry):
         for when in turns:
@@ -837,45 +893,10 @@
 
         source, view = table[1, t], table[2, t]
 
-        def take(condition, key, load):
-            @pl.when(condition)
-            def _():
-                cur[...] = jnp.where(source == key, load(), cur[...])
-
-        def take_any(condition, start, ref):
-            spot = source - start
-            held = ref.shape[0]
-
-            @pl.when(condition)
-            def _():
-                value = ref[jnp.clip(spot, 0, held - 1)]
-                cur[...] = jnp.where((spot >= 0) & (spot < held), value, cur[...])
-
-        @pl.when(t < 2)
-        def _():
-            cur[...] = keys[jnp.minimum(t, 1)]
-
-        take_any(t >= 2, 0, near)
-        for j, ref in enumerate((b0, b1)):
-            take_any((t >= 2) & is_mid, PLAIN + j * views, ref)
-        take_any((t >= late[1]) & is_mid, PLAIN + 2 * views, b2)
-        take((t >= 2) & is_end, FREE, lambda: first_view[...])
-        for q in range(FAR - 2):
-            since = 2 if q < 3 else late[1]
-            take(
-                (t >= since) & (t < late[3]) & is_end, SLOTS + q,
-                functools.partial(far.__getitem__, q),
-            )
-        take_any((t >= late[3]) & is_end, SLOTS, far)
-        for k in range(WIDE - 1):
-            since = late[0] if k < 3 else (late[2] if k < 5 else late[3])
-            take((t >= since) & (t < late[4]), CROSS + k, functools.partial(wide.__getitem__, k))
-        take_any(t >= late[4], CROSS, wide)
-
         def store(cols, value):
             results[t, :, cols] = value
 
-        attend(lambda cols: queries[view, :, cols], cur[...], w_key, w_value, pair, store)
+        heads(lambda cols: queries[view, :, cols], pairs.at[source], features, store)
         return carry
 
     lax.fori_loop(0, entries + 2, entry, 0)
@@ -958,9 +979,8 @@
         out_specs=(vmem, smem),
         scratch_shapes=[
             *[pltpu.VMEM((features, features), half)] * 4,
-            *[slabs(views)] * 6,
-            pltpu.VMEM(slab, half),
-            slabs(FAR),
+            *[slabs(views)] * 3,
+            slabs(3 * views),
             slabs(WIDE),
             slabs(2),
             slabs(FAR),
@@ -973,8 +993,7 @@
             numbers(1, 7 * views),
             numbers(1, FAR + WIDE),
             numbers(3, entries + 2),
-            pltpu.VMEM(slab, half),
-            pltpu.VMEM((length, 2 * features), half),
+            pltpu.VMEM((KEYS + 2, length, 2 * features), half),
             pltpu.VMEM((entries + 2, *slab), jnp.float32),
             pltpu.SemaphoreType.DMA((4,)),
             pltpu.SemaphoreType.DMA((5 * views + FAR + WIDE + 16,)),
@@ -982,7 +1001,7 @@
             *[numbers(1, 1)] * (2 * (4 + 2 * rounds)),
         ],
         compiler_params=pltpu.CompilerParams(
-            collective_id=1, has_side_effects=True, vmem_limit_bytes=48 * 1024 * 1024
+            collective_id=1, has_side_effects=True, vmem_limit_bytes=50 * 1024 * 1024
         ),
         name="sublayer_quick",
     )(partners, counts, key_slot, tokens, *stay)

time: 98.6 us -> 101 us (1.024)
  the two profiles are of different devices: /device:TPU:0 before, /device:TPU:16 now
where the time goes in v5:
time: 101 us
  Pallas kernels  96.6 us (96%)
  local copies, waits for them, and re-layouts  2.92 us (3%)
  between operations  1.28 us (1%)
    pallas_call x1, Pallas kernels, quick(): pl.pallas_call(functools.partial(quick_kernel, degree), out_shape=(jax.Sh...  96.6 us
    unnamed x8, local copies, waits for them, and re-layouts  2.92 us

profile of v5, /device:TPU:16, one launch (start us, length us, event | category | flops | bytes accessed | tf_op | source)
XLA Modules:
  0.0 100.8 jit_solution(15807551927315822468)
XLA Ops:
  0.7 0.0 copy-start.1
  0.7 0.0 copy-start.2
  0.7 1.4 %copy.11.refs_3_ = bf16[4,196,768]{2,1,0:T(8,128)(2,1)S(1)} copy(bf16[4,196,768]{2,0,1:T(4,128)(2,1)} %param.10) | data formatting | bytes 2408448 | tf_op args[0]
  2.1 0.0 copy-done.1
  2.1 0.0 copy-done.2
  2.1 0.0 copy-start
  2.1 96.6 %sublayer_quick.1 = (bf16[4,196,768]{2,1,0:T(8,128)(2,1)S(1)}, s32[1,1]{1,0:T(1,128)}) custom-call(s32[4,4]{1,0:T(4,128)S(1)} %copy-done.1, s32[4]{0:T(128)S(1)} %copy-done.2, s32[1]{0:T(128)S(6)} %copy.16.refs_2_, bf16[4,196,768]{2,1,0:T(8,128)(2,1)S(1)} %copy.11.refs_3_, bf16[768,768]{1,0:T(8,128)(2,1)} %refs_4_.1, bf16[768,768]{1,0:T(8,128)(2,1)} %refs_5_.1, ...), custom_call_target="tpu_custom_call" | custom-call | tf_op jit(solution)/shard_map/sublayer_quick/pallas_call | solution.py:972
  99.3 0.0 copy-done
  99.3 1.5 %copy.13 = bf16[4,196,768]{2,0,1:T(4,128)(2,1)} copy(bf16[4,196,768]{2,1,0:T(8,128)(2,1)S(1)} %get-tuple-element.37) | data formatting | bytes 2408448
  (1 shorter events, 0.0 us)
Async XLA Ops:
  0.7 1.4 %copy-start.1 = (s32[4,4]{1,0:T(4,128)S(1)}, s32[4,4]{1,0:T(4,128)}, u32[]{:S(2)}) copy-start(s32[4,4]{1,0:T(4,128)} %refs_0_.1) | copy-start | bytes 196
  0.7 1.4 %copy-start.2 = (s32[4]{0:T(128)S(1)}, s32[4]{0:T(128)}, u32[]{:S(2)}) copy-start(s32[4]{0:T(128)} %refs_1_.1) | copy-start | bytes 52
  2.1 97.2 %copy-start = (bf16[4,196,768]{2,0,1:T(4,128)(2,1)S(1)}, bf16[4,196,768]{2,0,1:T(4,128)(2,1)}, u32[]{:S(2)}) copy-start(bf16[4,196,768]{2,0,1:T(4,128)(2,1)} %param.10) | copy-start | bytes 3612676

commit v6 on v5

--- a/solution.py
+++ b/solution.py
@@ -446,10 +446,10 @@
 def quick_kernel(degree, *refs):
     partners, counts, key_slot, tokens, wq_in, wk_in, wv_in, wo_in, out_ref, flag_ref = refs[:10]
     w_query, w_key, w_value, w_out = refs[10:14]
-    own, queries, near, landing, wide, keys, far_out, wide_out, key_out = refs[14:23]
-    ask, asked, union, codes, sources, picks, table, pairs, results = refs[23:32]
-    load_sem, send_sem, recv_sem = refs[32:35]
-    notes = refs[35:]
+    own, queries, arrived, far_out, wide_out, key_out = refs[14:20]
+    ask, asked, union, codes, sources, picks, table, pairs, results = refs[20:29]
+    load_sem, send_sem, recv_sem = refs[29:32]
+    notes = refs[32:]
     views, length, features = tokens.shape
     members, groups = lax.axis_size("member"), lax.axis_size("group")
     entries = views * degree
@@ -467,8 +467,9 @@
     below = {"group": lax.rem(group + groups - 1, groups)}
     key_view = key_slot[0]
     cells = 7 * views
-    b0, b1, b2 = (landing.at[pl.ds(i * views, views)] for i in range(3))
-    first_view, far = landing.at[pl.ds(0, 1)], landing.at[pl.ds(1, FAR)]
+    near, b0, b1, b2 = (arrived.at[pl.ds(i * views, views)] for i in range(4))
+    first_view, far = arrived.at[pl.ds(FREE, 1)], arrived.at[pl.ds(SLOTS, FAR)]
+    wide, keys = arrived.at[pl.ds(CROSS, WIDE)], arrived.at[pl.ds(KEYS, 2)]
     names = {}
 
     def number(kind, name):
@@ -794,112 +795,118 @@
     lax.fori_loop(0, entries + 2, sort, 0)
     loads[1].wait()
     loads[2].wait()
-    for i in range(2):
-        key_send(i).wait_recv()
-
-    def learn(place, ref, start, count):
-        def one(i, carry):
-            rows = ref[start + i]
-            pairs[place + i, :, :features] = project(rows, w_key[...]).astype(jnp.bfloat16)
-            pairs[place + i, :, features:] = project(rows, w_value[...]).astype(jnp.bfloat16)
-            return carry
-
-        lax.fori_loop(0, count, one, 0)
-
-    def learn_far(first, last):
-        @pl.when(is_end)
-        def _():
-            learn(SLOTS + first, far, first, last - first)
-
-    def learn_last(first, last):
-        @pl.when(is_mid)
-        def _():
-            learn(PLAIN + 2 * views + first, b2, first, last - first)
-
-    learn(KEYS, keys, 0, 2)
-
-    late = [2 + max(0, entries - n) for n in (15, 12, 9, 7, 3)]
-    turns = {
-        1: [lambda: far_turn(1)],
-        2: [lambda: far_turn(2), lambda: far_turn(3), lambda: far_turn(4)]
-        + [functools.partial(far_arrive, q) for q in range(2)],
-        late[0]: [lambda: far_turn(5), lambda: wide_turn(1), lambda: far_turn(6)]
-        + [lambda: wide_turn(2)],
-        late[1]: [lambda: far_turn(8), lambda: wide_turn(4), lambda: note_step(3)],
-        late[2]: [lambda: wide_turn(5)],
-        late[3]: [lambda: wide_turn(6)],
-        late[4]: [],
-    }
-    for i in range(1, rounds + 1):
-        turns[late[3] + i] = [functools.partial(note_step, 4 + i)]
-
-    def events(t):
-        for turn in turns[t]:
-            turn()
-        if t == 2:
+    plan = []
+
+    def do(*actions):
+        plan.append([list(actions), None, None])
+
+    def learn(end, mid):
+        plan.append([[], (end, mid), None])
+
+    def attends(first, last, *actions):
+        for r in range(first, last):
+            plan.append([[], None, r + 2])
+        for i, action in enumerate(actions):
+            plan[i - len(actions)][0].append(action)
+
+    def key_arrive():
+        for i in range(2):
+            key_send(i).wait_recv()
+
+    def near_arrive(v):
+        to_near(v).wait_recv()
+        if v == 0:
             @pl.when(is_end)
             def _():
                 own_out().wait_recv()
-
-            for v in range(views):
-                to_near(v).wait_recv()
-            wide_turn(0)
-            note_step(1)
-            learn(0, near, 0, views)
-
-            @pl.when(is_end)
-            def _():
-                learn(FREE, first_view, 0, 1)
-
-            @pl.when(is_mid)
-            def _():
-                learn(PLAIN, b0, 0, views)
-                learn(PLAIN + views, b1, 0, views)
-
-            learn_far(0, 3)
-        if t == late[0]:
-            learn_far(3, 5)
-            learn_last(0, 2)
-            for k in range(3):
-                wide_send(k).wait_recv()
-            far_turn(7)
-            wide_turn(3)
-            note_step(2)
-            learn(CROSS, wide, 0, 3)
-            learn_far(5, 6)
-            learn_last(2, 3)
-        if t == late[1]:
-            learn_far(6, 7)
-            learn_last(3, 4)
-        if t == late[2]:
-            wide_send(3).wait_recv()
-            wide_send(4).wait_recv()
-            learn(CROSS + 3, wide, 3, 2)
-            learn_far(7, 8)
-        if t == late[3]:
-            wide_send(5).wait_recv()
-            note_step(4)
-            learn(CROSS + 5, wide, 5, 1)
-            learn_far(8, 9)
-        if t == late[4]:
-            wide_send(6).wait_recv()
-            learn(CROSS + 6, wide, 6, 1)
-
-    def entry(t, carry):
-        for when in turns:
-            @pl.when(t == when)
-            def _():
-                events(when)
-
-        source, view = table[1, t], table[2, t]
-
+        elif v < views - 1:
+            far_arrive(v - 1)
+
+    def wide_arrive(k):
+        wide_send(k).wait_recv()
+
+    run = functools.partial
+    for v in range(views):
+        do(run(far_turn, v + 1), run(near_arrive, v))
+        if v == views - 1:
+            do(run(wide_turn, 0))
+        learn(v, v)
+        learn(FREE + v, PLAIN + v)
+        learn(None, PLAIN + views + v)
+        if v == 0:
+            do(key_arrive)
+            learn(KEYS, KEYS)
+            learn(KEYS + 1, KEYS + 1)
+            attends(-2, -1)
+        if v == 1:
+            attends(-1, 0)
+    bounds = [max(0, entries - n) for n in (15, 15, 15, 12, 9, 7, 3, 0)]
+    attends(0, bounds[0])
+    for k in range(1, WIDE):
+        if views + k < FAR:
+            do(run(far_turn, views + k))
+        do(run(wide_turn, k))
+        if k < 5:
+            do(run(note_step, k - 1) if k > 1 else (lambda: None))
+        learn(FREE + views - 1 + k, PLAIN + 2 * views + k - 1 if k <= views else None)
+        do(run(wide_arrive, k - 1))
+        learn(CROSS + k - 1, CROSS + k - 1)
+        attends(bounds[k - 1], bounds[k])
+    plan[-3][0].append(run(note_step, 4))
+    for i in range(1, rounds + 1):
+        plan[i - 3][0].append(run(note_step, 4 + i))
+    do(run(wide_arrive, WIDE - 1))
+    learn(CROSS + WIDE - 1, CROSS + WIDE - 1)
+    attends(bounds[WIDE - 1], bounds[WIDE])
+    steps = []
+    waiting = []
+    for actions, views_to_learn, r in plan:
+        waiting += actions
+        if views_to_learn is not None or r is not None:
+            steps.append((waiting, views_to_learn, r))
+            waiting = []
+
+    def number_at(u, values):
+        value = jnp.int32(-1)
+        for i, wanted in enumerate(values):
+            if wanted is not None:
+                value = jnp.where(u == i, wanted, value)
+        return value
+
+    def store_to(t):
         def store(cols, value):
             results[t, :, cols] = value
 
-        heads(lambda cols: queries[view, :, cols], pairs.at[source], features, store)
+        return store
+
+    def step(u, carry):
+        for i, (actions, _, _) in enumerate(steps):
+            if actions:
+                @pl.when(u == i)
+                def _():
+                    for action in actions:
+                        action()
+
+        end = number_at(u, [pick and pick[0] for _, pick, _ in steps])
+        mid = number_at(u, [pick and pick[1] for _, pick, _ in steps])
+        place = jnp.where(is_end, end, mid)
+
+        @pl.when(place >= 0)
+        def _():
+            rows = arrived[place]
+            pairs[place, :, :features] = project(rows, w_key[...]).astype(jnp.bfloat16)
+            pairs[place, :, features:] = project(rows, w_value[...]).astype(jnp.bfloat16)
+
+        t = number_at(u, [r for _, _, r in steps])
+
+        @pl.when(t >= 0)
+        def _():
+            source, view = table[1, t], table[2, t]
+            heads(lambda cols: queries[view, :, cols], pairs.at[source], features, store_to(t))
+
         return carry
 
-    lax.fori_loop(0, entries + 2, entry, 0)
+    lax.fori_loop(0, len(steps), step, 0)
     loads[3].wait()
     for v in range(views):
         is_key = (key_view == v).astype(jnp.int32)
@@ -979,10 +986,8 @@
         out_specs=(vmem, smem),
         scratch_shapes=[
             *[pltpu.VMEM((features, features), half)] * 4,
-            *[slabs(views)] * 3,
-            slabs(3 * views),
-            slabs(WIDE),
-            slabs(2),
+            *[slabs(views)] * 2,
+            slabs(KEYS + 2),
             slabs(FAR),
             slabs(WIDE),
             pltpu.VMEM(slab, half),

time: 101 us -> 96.9 us (0.959)
  Pallas kernels: 96.6 us -> 92.4 us
    pallas_call x1, Pallas kernels: 96.6 us -> 92.4 us  [quick(): pl.pallas_call(functools.partial(quick_kernel, degree), out_shape=(jax.Sh...]
where the time goes in v6:
time: 96.9 us
  Pallas kernels  92.4 us (95%)
  local copies, waits for them, and re-layouts  2.92 us (3%)
  between operations  1.28 us (1%)
    pallas_call x1, Pallas kernels, quick(): pl.pallas_call(functools.partial(quick_kernel, degree), out_shape=(jax.Sh...  92.4 us
    unnamed x8, local copies, waits for them, and re-layouts  2.92 us

profile of v6, /device:TPU:16, one launch (start us, length us, event | category | flops | bytes accessed | tf_op | source)
XLA Modules:
  0.0 96.9 jit_solution(8365059297207667681)
XLA Ops:
  0.7 0.0 copy-start.1
  0.7 0.0 copy-start.2
  0.7 1.4 %copy.11.refs_3_ = bf16[4,196,768]{2,1,0:T(8,128)(2,1)S(1)} copy(bf16[4,196,768]{2,0,1:T(4,128)(2,1)} %param.10) | data formatting | bytes 2408448 | tf_op args[0]
  2.1 0.0 copy-done.1
  2.1 0.0 copy-done.2
  2.1 0.0 copy-start
  2.1 92.4 %sublayer_quick.1 = (bf16[4,196,768]{2,1,0:T(8,128)(2,1)S(1)}, s32[1,1]{1,0:T(1,128)}) custom-call(s32[4,4]{1,0:T(4,128)S(1)} %copy-done.1, s32[4]{0:T(128)S(1)} %copy-done.2, s32[1]{0:T(128)S(6)} %copy.16.refs_2_, bf16[4,196,768]{2,1,0:T(8,128)(2,1)S(1)} %copy.11.refs_3_, bf16[768,768]{1,0:T(8,128)(2,1)} %refs_4_.1, bf16[768,768]{1,0:T(8,128)(2,1)} %refs_5_.1, ...), custom_call_target="tpu_custom_call" | custom-call | tf_op jit(solution)/shard_map/sublayer_quick/pallas_call | solution.py:979
  95.1 0.0 copy-done
  95.1 0.2 conditional.1
  95.4 1.5 %copy.13 = bf16[4,196,768]{2,0,1:T(4,128)(2,1)} copy(bf16[4,196,768]{2,1,0:T(8,128)(2,1)S(1)} %get-tuple-element.37) | data formatting | bytes 2408448
Async XLA Ops:
  0.7 1.4 %copy-start.1 = (s32[4,4]{1,0:T(4,128)S(1)}, s32[4,4]{1,0:T(4,128)}, u32[]{:S(2)}) copy-start(s32[4,4]{1,0:T(4,128)} %refs_0_.1) | copy-start | bytes 196
  0.7 1.4 %copy-start.2 = (s32[4]{0:T(128)S(1)}, s32[4]{0:T(128)}, u32[]{:S(2)}) copy-start(s32[4]{0:T(128)} %refs_1_.1) | copy-start | bytes 52
  2.1 93.0 %copy-start = (bf16[4,196,768]{2,0,1:T(4,128)(2,1)S(1)}, bf16[4,196,768]{2,0,1:T(4,128)(2,1)}, u32[]{:S(2)}) copy-start(bf16[4,196,768]{2,0,1:T(4,128)(2,1)} %param.10) | copy-start | bytes 3612676

commit v7 on v6

--- a/solution.py
+++ b/solution.py
@@ -795,25 +795,34 @@
     lax.fori_loop(0, entries + 2, sort, 0)
     loads[1].wait()
     loads[2].wait()
-    plan = []
-
-    def do(*actions):
-        plan.append([list(actions), None, None])
-
-    def learn(end, mid):
-        plan.append([[], (end, mid), None])
-
-    def attends(first, last, *actions):
-        for r in range(first, last):
-            plan.append([[], None, r + 2])
-        for i, action in enumerate(actions):
-            plan[i - len(actions)][0].append(action)
-
-    def key_arrive():
-        for i in range(2):
-            key_send(i).wait_recv()
-
-    def near_arrive(v):
+    def learn(first, stride, count):
+        def one(i, carry):
+            place = first + stride * i
+            rows = arrived[place]
+            pairs[place, :, :features] = project(rows, w_key[...]).astype(jnp.bfloat16)
+            pairs[place, :, features:] = project(rows, w_value[...]).astype(jnp.bfloat16)
+            return carry
+
+        lax.fori_loop(0, count, one, 0)
+
+    def attends(first, last):
+        def one(t, carry):
+            source, view = table[1, t], table[2, t]
+
+            def store(cols, value):
+                results[t, :, cols] = value
+
+            heads(lambda cols: queries[view, :, cols], pairs.at[source], features, store)
+            return carry
+
+        if last > first:
+            lax.fori_loop(first + 2, last + 2, one, 0)
+
+    def wide_arrive(k):
+        wide_send(k).wait_recv()
+
+    for v in range(views):
+        far_turn(v + 1)
         to_near(v).wait_recv()
         if v == 0:
             @pl.when(is_end)
@@ -821,92 +830,40 @@
                 own_out().wait_recv()
         elif v < views - 1:
             far_arrive(v - 1)
-
-    def wide_arrive(k):
-        wide_send(k).wait_recv()
-
-    run = functools.partial
-    for v in range(views):
-        do(run(far_turn, v + 1), run(near_arrive, v))
-        if v == views - 1:
-            do(run(wide_turn, 0))
-        learn(v, v)
-        learn(FREE + v, PLAIN + v)
-        learn(None, PLAIN + views + v)
+        else:
+            wide_turn(0)
+        learn(v, views, jnp.where(is_end, 2, 3))
         if v == 0:
-            do(key_arrive)
-            learn(KEYS, KEYS)
-            learn(KEYS + 1, KEYS + 1)
-            attends(-2, -1)
+            for i in range(2):
+                key_send(i).wait_recv()
+            learn(KEYS, 1, 2)
         if v == 1:
-            attends(-1, 0)
+            attends(-2, 0)
     bounds = [max(0, entries - n) for n in (15, 15, 15, 12, 9, 7, 3, 0)]
     attends(0, bounds[0])
     for k in range(1, WIDE):
         if views + k < FAR:
-            do(run(far_turn, views + k))
-        do(run(wide_turn, k))
-        if k < 5:
-            do(run(note_step, k - 1) if k > 1 else (lambda: None))
-        learn(FREE + views - 1 + k, PLAIN + 2 * views + k - 1 if k <= views else None)
-        do(run(wide_arrive, k - 1))
-        learn(CROSS + k - 1, CROSS + k - 1)
-        attends(bounds[k - 1], bounds[k])
-    plan[-3][0].append(run(note_step, 4))
-    for i in range(1, rounds + 1):
-        plan[i - 3][0].append(run(note_step, 4 + i))
-    do(run(wide_arrive, WIDE - 1))
-    learn(CROSS + WIDE - 1, CROSS + WIDE - 1)
+            far_turn(views + k)
+        wide_turn(k)
+        if 1 < k < 5:
+            note_step(k - 1)
+        there = 1 if k <= views else 0
+        landed = jnp.where(is_end, FREE + views - 1 + k, PLAIN + 2 * views + k - 1)
+        learn(landed, 0, jnp.where(is_end, 1, there))
+        wide_arrive(k - 1)
+        learn(CROSS + k - 1, 0, 1)
+        if k < WIDE - 1:
+            attends(bounds[k - 1], bounds[k])
+    middle = (bounds[WIDE - 2] + bounds[WIDE - 1]) // 2
+    attends(bounds[WIDE - 2], middle)
+    note_step(4)
+    attends(middle, bounds[WIDE - 1])
+    wide_arrive(WIDE - 1)
+    learn(CROSS + WIDE - 1, 0, 1)
+    for i in range(1, rounds):
+        note_step(4 + i)
     attends(bounds[WIDE - 1], bounds[WIDE])
-    steps = []
-    waiting = []
-    for actions, views_to_learn, r in plan:
-        waiting += actions
-        if views_to_learn is not None or r is not None:
-            steps.append((waiting, views_to_learn, r))
-            waiting = []
-
-    def number_at(u, values):
-        value = jnp.int32(-1)
-        for i, wanted in enumerate(values):
-            if wanted is not None:
-                value = jnp.where(u == i, wanted, value)
-        return value
-
-    def store_to(t):
-        def store(cols, value):
-            results[t, :, cols] = value
-
-        return store
-
-    def step(u, carry):
-        for i, (actions, _, _) in enumerate(steps):
-            if actions:
-                @pl.when(u == i)
-                def _():
-                    for action in actions:
-                        action()
-
-        end = number_at(u, [pick and pick[0] for _, pick, _ in steps])
-        mid = number_at(u, [pick and pick[1] for _, pick, _ in steps])
-        place = jnp.where(is_end, end, mid)
-
-        @pl.when(place >= 0)
-        def _():
-            rows = arrived[place]
-            pairs[place, :, :features] = project(rows, w_key[...]).astype(jnp.bfloat16)
-            pairs[place, :, features:] = project(rows, w_value[...]).astype(jnp.bfloat16)
-
-        t = number_at(u, [r for _, _, r in steps])
-
-        @pl.when(t >= 0)
-        def _():
-            source, view = table[1, t], table[2, t]
-            heads(lambda cols: queries[view, :, cols], pairs.at[source], features, store_to(t))
-
-        return carry
-
-    lax.fori_loop(0, len(steps), step, 0)
+    note_step(4 + rounds)
     loads[3].wait()
     for v in range(views):
         is_key = (key_view == v).astype(jnp.int32)

time: 96.9 us -> 94.3 us (0.973)
  the two profiles are of different devices: /device:TPU:16 before, /device:TPU:0 now
where the time goes in v7:
time: 94.3 us; the launch traced here: 92.8 us
  Pallas kernels  88.6 us (94%)
  local copies, waits for them, and re-layouts  2.92 us (3%)
  between operations  1.28 us (1%)
    pallas_call x1, Pallas kernels, quick(): pl.pallas_call(functools.partial(quick_kernel, degree), out_shape=(jax.Sh...  88.6 us
    unnamed x8, local copies, waits for them, and re-layouts  2.92 us

profile of v7, /device:TPU:0, one launch (start us, length us, event | category | flops | bytes accessed | tf_op | source)
XLA Modules:
  0.0 92.8 jit_solution(11086864617963217084)
XLA Ops:
  0.7 0.0 copy-start.1
  0.7 0.0 copy-start.2
  0.7 1.4 %copy.11.refs_3_ = bf16[4,196,768]{2,1,0:T(8,128)(2,1)S(1)} copy(bf16[4,196,768]{2,0,1:T(4,128)(2,1)} %param.10) | data formatting | bytes 2408448 | tf_op args[0]
  2.1 0.0 copy-done.1
  2.1 0.0 copy-done.2
  2.1 0.0 copy-start
  2.1 88.6 %sublayer_quick.1 = (bf16[4,196,768]{2,1,0:T(8,128)(2,1)S(1)}, s32[1,1]{1,0:T(1,128)}) custom-call(s32[4,4]{1,0:T(4,128)S(1)} %copy-done.1, s32[4]{0:T(128)S(1)} %copy-done.2, s32[1]{0:T(128)S(6)} %copy.16.refs_2_, bf16[4,196,768]{2,1,0:T(8,128)(2,1)S(1)} %copy.11.refs_3_, bf16[768,768]{1,0:T(8,128)(2,1)} %refs_4_.1, bf16[768,768]{1,0:T(8,128)(2,1)} %refs_5_.1, ...), custom_call_target="tpu_custom_call" | custom-call | tf_op jit(solution)/shard_map/sublayer_quick/pallas_call | solution.py:936
  91.3 0.0 copy-done
  91.3 1.5 %copy.13 = bf16[4,196,768]{2,0,1:T(4,128)(2,1)} copy(bf16[4,196,768]{2,1,0:T(8,128)(2,1)S(1)} %get-tuple-element.37) | data formatting | bytes 2408448
  (1 shorter events, 0.0 us)
Async XLA Ops:
  0.7 1.4 %copy-start.1 = (s32[4,4]{1,0:T(4,128)S(1)}, s32[4,4]{1,0:T(4,128)}, u32[]{:S(2)}) copy-start(s32[4,4]{1,0:T(4,128)} %refs_0_.1) | copy-start | bytes 196
  0.7 1.4 %copy-start.2 = (s32[4]{0:T(128)S(1)}, s32[4]{0:T(128)}, u32[]{:S(2)}) copy-start(s32[4]{0:T(128)} %refs_1_.1) | copy-start | bytes 52
  2.1 89.2 %copy-start = (bf16[4,196,768]{2,0,1:T(4,128)(2,1)S(1)}, bf16[4,196,768]{2,0,1:T(4,128)(2,1)}, u32[]{:S(2)}) copy-start(bf16[4,196,768]{2,0,1:T(4,128)(2,1)} %param.10) | copy-start | bytes 3612676

commit v8 on v7

--- a/solution.py
+++ b/solution.py
@@ -438,7 +438,7 @@
     )(partners, counts, key_slot, tokens, *stay)
 
 
-FAR, WIDE = 9, 7
+NEAR, FAR, WIDE, EARLY = 3, 9, 7, 3
 FREE, SLOTS, PLAIN, CROSS = 4, 5, 4, 16
 KEYS = CROSS + WIDE
 
@@ -446,10 +446,10 @@
 def quick_kernel(degree, *refs):
     partners, counts, key_slot, tokens, wq_in, wk_in, wv_in, wo_in, out_ref, flag_ref = refs[:10]
     w_query, w_key, w_value, w_out = refs[10:14]
-    own, queries, arrived, far_out, wide_out, key_out = refs[14:20]
-    ask, asked, union, codes, sources, picks, table, pairs, results = refs[20:29]
-    load_sem, send_sem, recv_sem = refs[29:32]
-    notes = refs[32:]
+    own, queries, arrived, near_out, far_out, wide_out, key_out = refs[14:21]
+    ask, asked, union, codes, sources, picks, table, pairs, results = refs[21:30]
+    load_sem, send_sem, recv_sem = refs[30:33]
+    notes = refs[33:]
     views, length, features = tokens.shape
     members, groups = lax.axis_size("member"), lax.axis_size("group")
     entries = views * degree
@@ -467,6 +467,8 @@
     below = {"group": lax.rem(group + groups - 1, groups)}
     key_view = key_slot[0]
     cells = 7 * views
+    cut = length // 32 * 16
+    halves = (pl.ds(0, cut), pl.ds(cut, length - cut))
     near, b0, b1, b2 = (arrived.at[pl.ds(i * views, views)] for i in range(4))
     first_view, far = arrived.at[pl.ds(FREE, 1)], arrived.at[pl.ds(SLOTS, FAR)]
     wide, keys = arrived.at[pl.ds(CROSS, WIDE)], arrived.at[pl.ds(KEYS, 2)]
@@ -481,8 +483,8 @@
             recv_sem=recv_sem.at[number(1, landing)], device_id=device, device_id_type=MESH,
         )
 
-    def to_near(v):
-        return remote(("near", v), own.at[v], near.at[v], ("near", v), beside)
+    def near_send(k):
+        return remote(("near", k), near_out.at[k], near.at[k], ("near", k), beside)
 
     def own_to_b1(v):
         return remote(("in", v), own.at[v], b1.at[v], ("b1", v), inner)
@@ -496,11 +498,13 @@
     def own_out():
         return remote("free", own.at[0], first_view.at[0], "free", outer)
 
-    def far_send(q):
-        return remote(("far", q), far_out.at[q], far.at[q], ("far", q), outer)
-
-    def wide_send(k):
-        return remote(("wide", k), wide_out.at[k], wide.at[k], ("wide", k), beside)
+    def far_send(q, p):
+        rows = halves[p]
+        return remote(("far", q, p), far_out.at[q, rows], far.at[q, rows], ("far", q, p), outer)
+
+    def wide_send(k, p):
+        rows = halves[p]
+        return remote(("wide", k, p), wide_out.at[k, rows], wide.at[k, rows], ("wide", k, p), beside)
 
     def key_send(i):
         return remote(("key", i), key_out, keys.at[i], ("key", i), below if i else above)
@@ -544,7 +548,7 @@
         across = (lax.rem(peer, ROW) != side).astype(jnp.int32)
         block = jnp.where(there == here, 0, 1 + 2 * turn + across)
         live = lax.rem(e, degree) < counts[lax.div(e, degree)]
-        codes[0, e] = jnp.where(live, block * views + lax.rem(partner, views), 0)
+        codes[0, e] = jnp.where(live, block * views + lax.rem(partner, views), -1)
         return carry
 
     lax.fori_loop(0, entries, read, 0)
@@ -571,7 +575,6 @@
     for v in range(views):
         if v:
             own[v] = layer_norm(tokens[v]).astype(jnp.bfloat16)
-        to_near(v).start()
 
         @pl.when(is_mid)
         def _():
@@ -598,6 +601,14 @@
         for v in range(views):
             own_to_b1(v).start()
 
+    near_flags = [asked[0, v] for v in range(views)]
+    near_spots = [sum(near_flags[:v]) for v in range(views)]
+    for k in range(NEAR):
+        pick = jnp.int32(0)
+        for v in range(views):
+            pick = jnp.where((near_flags[v] == 1) & (near_spots[v] == k), v, pick)
+        near_out[k] = own[pick]
+        near_send(k).start()
     loads[0].wait()
     for v in range(views):
         queries[v] = project(own[v], w_query[...]).astype(jnp.bfloat16) * jnp.bfloat16(size**-0.5)
@@ -618,6 +629,9 @@
 
     far_ready = [0] * views + [v + 1 for v in range(views)] + [v + 1 + views for v in range(views)]
 
+    mid_ready = [max(0, v - 2) for v in range(views)] + [max(0, v - 1) for v in range(views)]
+    mid_ready += [v + EARLY for v in range(views)]
+
     def far_slots(flags):
         spots, last = line_up(flags[1:], far_ready[1:])
         return [jnp.int32(-1)] + spots, last
@@ -625,8 +639,7 @@
     def wide_slots(flags, behind):
         ready = []
         for c in range(count):
-            late = 0 if c < 2 * views else c - 2 * views + 1
-            ready.append(jnp.where(is_end, jnp.maximum(behind[c] - 2, 0), late))
+            ready.append(jnp.where(is_end, jnp.maximum(behind[c] - 2, 0), mid_ready[c]))
         return line_up(flags, ready)
 
     def found(c, spots):
@@ -649,7 +662,7 @@
             pick = jnp.where((out_flags[c] == 1) & (my_wide[c] == k), found(c, my_far), pick)
         picks[0, FAR + k] = pick
     for v in range(views):
-        sources[0, v] = v
+        sources[0, v] = sum(ask[0, other] for other in range(v)) if v else 0
     for c in range(count):
         sources[0, (1 + 2 * (c // views)) * views + c % views] = found(c, my_far)
         sources[0, (2 + 2 * (c // views)) * views + c % views] = CROSS + beside_wide[c]
@@ -672,7 +685,8 @@
             (2 * views + v, functools.partial(view_of, b2, v)) for v in range(views) if v + views < q
         ]
         far_out[q] = choose(picks[0, q], options)
-        far_send(q).start()
+        for p in range(2):
+            far_send(q, p).start()
 
     def far_turn(q):
         @pl.when(is_mid)
@@ -682,40 +696,39 @@
             if q > views:
                 b1_in(q - 1 - views).wait_recv()
             far_stage(q)
-            if 1 <= q <= views:
-                own_to_b1(q - 1).wait_recv()
-                b1_in(q - 1).start()
-
-    def wide_stage(k):
-        choice = picks[0, FAR + k]
-
+            if 2 <= q <= views + 1:
+                own_to_b1(q - 2).wait_recv()
+                b1_in(q - 2).start()
+
+    def wide_end(k, p):
         @pl.when(is_end)
         def _():
-            options = [(FREE, lambda: first_view[0])]
-            options += [(SLOTS + q, functools.partial(view_of, far, q)) for q in range(k + 3)]
-            wide_out[k] = choose(choice, options)
-
+            far_send(k + 2, p).wait_recv()
+            options = [(FREE, lambda: first_view[0, halves[p]])]
+            options += [
+                (SLOTS + q, functools.partial(view_of, far, (q, halves[p]))) for q in range(k + 3)
+            ]
+            wide_out[k, halves[p]] = choose(picks[0, FAR + k], options)
+            wide_send(k, p).start()
+
+    def wide_mid(k):
         @pl.when(is_mid)
         def _():
-            options = [(PLAIN + v, functools.partial(view_of, b0, v)) for v in range(views)]
-            options += [(PLAIN + views + v, functools.partial(view_of, b1, v)) for v in range(views)]
-            options += [
-                (PLAIN + 2 * views + v, functools.partial(view_of, b2, v))
-                for v in range(views)
-                if v < k
+            held = b0, b1, b2
+            options = [
+                (PLAIN + c, functools.partial(view_of, held[c // views], c % views))
+                for c in range(count)
+                if mid_ready[c] <= k
             ]
-            wide_out[k] = choose(choice, options)
-
-        wide_send(k).start()
+            wide_out[k] = choose(picks[0, FAR + k], options)
+            for p in range(2):
+                wide_send(k, p).start()
 
     def far_arrive(q):
         @pl.when(is_end)
         def _():
-            far_send(q).wait_recv()
-
-    def wide_turn(k):
-        far_arrive(k + 2)
-        wide_stage(k)
+            for p in range(2):
+                far_send(q, p).wait_recv()
 
     def note_value(i, value):
         notes[2 * i][0, 0] = value
@@ -789,15 +802,18 @@
             match = table[0, e] == r
             cell = jnp.where(match, codes[0, e], cell)
             view = jnp.where(match, e // degree, view)
-        table[1, r], table[2, r] = jnp.where(r < 2, KEYS + r, sources[0, cell]), view
+        source = jnp.where(cell < 0, KEYS, sources[0, jnp.maximum(cell, 0)])
+        table[1, r], table[2, r] = jnp.where(r < 2, KEYS + r, source), view
         return carry
 
     lax.fori_loop(0, entries + 2, sort, 0)
     loads[1].wait()
     loads[2].wait()
-    def learn(first, stride, count):
+    def learn(places, count):
         def one(i, carry):
-            place = first + stride * i
+            place = places[0]
+            for turn in range(1, len(places)):
+                place = jnp.where(i == turn, places[turn], place)
             rows = arrived[place]
             pairs[place, :, :features] = project(rows, w_key[...]).astype(jnp.bfloat16)
             pairs[place, :, features:] = project(rows, w_value[...]).astype(jnp.bfloat16)
@@ -819,50 +835,71 @@
             lax.fori_loop(first + 2, last + 2, one, 0)
 
     def wide_arrive(k):
-        wide_send(k).wait_recv()
+        for p in range(2):
+            wide_send(k, p).wait_recv()
+        learn([CROSS + k], 1)
 
     for v in range(views):
         far_turn(v + 1)
-        to_near(v).wait_recv()
-        if v == 0:
+        if v == views - 1:
+            wide_end(0, 0)
+            wide_end(0, 1)
+        elif v:
+            far_arrive(v - 1)
+        else:
             @pl.when(is_end)
             def _():
                 own_out().wait_recv()
-        elif v < views - 1:
-            far_arrive(v - 1)
-        else:
-            wide_turn(0)
-        learn(v, views, jnp.where(is_end, 2, 3))
+
+        if v >= views - 2:
+            wide_mid(v - views + 2)
+        places = [FREE + v]
+        if v < NEAR:
+            near_send(v).wait_recv()
+            places = [v, FREE + v]
+        more = [PLAIN + views + v - 1] if v else []
+        learn(places + more, jnp.where(is_end, len(places), len(places + more)))
         if v == 0:
             for i in range(2):
                 key_send(i).wait_recv()
-            learn(KEYS, 1, 2)
+            learn([KEYS, KEYS + 1], 2)
         if v == 1:
             attends(-2, 0)
-    bounds = [max(0, entries - n) for n in (15, 15, 15, 12, 9, 7, 3, 0)]
+    bounds = [max(0, entries - n) for n in (15, 12, 9, 7, 6, 3, 0)]
     attends(0, bounds[0])
+    inside = {3: (bounds[0], bounds[0] + 1), 5: (bounds[2] - 1, bounds[2]), 6: (bounds[3], bounds[4])}
+    after = {3: (bounds[0] + 1, bounds[1]), 4: (bounds[1], bounds[2] - 1), 5: (bounds[2], bounds[3]),
+             6: (bounds[4], bounds[5])}
     for k in range(1, WIDE):
+        wide_end(k, 0)
+        if k >= EARLY:
+            wide_mid(k)
         if views + k < FAR:
             far_turn(views + k)
-        wide_turn(k)
+        if k == 1:
+            wide_mid(2)
+        wide_arrive(k - 1)
+        attends(*inside.get(k, (0, 0)))
+        wide_end(k, 1)
         if 1 < k < 5:
             note_step(k - 1)
+        landed = jnp.where(is_end, FREE + views - 1 + k, PLAIN + 2 * views + k - 1)
         there = 1 if k <= views else 0
-        landed = jnp.where(is_end, FREE + views - 1 + k, PLAIN + 2 * views + k - 1)
-        learn(landed, 0, jnp.where(is_end, 1, there))
-        wide_arrive(k - 1)
-        learn(CROSS + k - 1, 0, 1)
-        if k < WIDE - 1:
-            attends(bounds[k - 1], bounds[k])
-    middle = (bounds[WIDE - 2] + bounds[WIDE - 1]) // 2
-    attends(bounds[WIDE - 2], middle)
-    note_step(4)
-    attends(middle, bounds[WIDE - 1])
+        if k == 1:
+            learn([landed, PLAIN + 2 * views - 1], jnp.where(is_end, 1, 2))
+        else:
+            learn([landed], jnp.where(is_end, 1, there))
+        if k == WIDE - 1:
+            first, last = after[k]
+            attends(first, last - 1)
+            note_step(4)
+            attends(last - 1, last)
+        else:
+            attends(*after.get(k, (0, 0)))
     wide_arrive(WIDE - 1)
-    learn(CROSS + WIDE - 1, 0, 1)
     for i in range(1, rounds):
         note_step(4 + i)
-    attends(bounds[WIDE - 1], bounds[WIDE])
+    attends(bounds[5], bounds[6])
     note_step(4 + rounds)
     loads[3].wait()
     for v in range(views):
@@ -879,8 +916,6 @@
         ).astype(out_ref.dtype)
 
     for v in range(views):
-        to_near(v).wait_send()
-
         @pl.when(is_end)
         def _():
             own_to_b1(v).wait_send()
@@ -894,7 +929,8 @@
     def _():
         own_out().wait_send()
         for q in range(FAR):
-            far_send(q).wait_send()
+            for p in range(2):
+                far_send(q, p).wait_send()
         note(2, inner).wait_send()
         note(3, outer).wait_send()
 
@@ -904,7 +940,10 @@
         note(1, inner).wait_send()
 
     for k in range(WIDE):
-        wide_send(k).wait_send()
+        for p in range(2):
+            wide_send(k, p).wait_send()
+    for k in range(NEAR):
+        near_send(k).wait_send()
     for i in range(2):
         key_send(i).wait_send()
     ask_send().wait_send()
@@ -945,6 +984,7 @@
             *[pltpu.VMEM((features, features), half)] * 4,
             *[slabs(views)] * 2,
             slabs(KEYS + 2),
+            slabs(NEAR),
             slabs(FAR),
             slabs(WIDE),
             pltpu.VMEM(slab, half),
@@ -958,8 +998,8 @@
             pltpu.VMEM((KEYS + 2, length, 2 * features), half),
             pltpu.VMEM((entries + 2, *slab), jnp.float32),
             pltpu.SemaphoreType.DMA((4,)),
-            pltpu.SemaphoreType.DMA((5 * views + FAR + WIDE + 16,)),
-            pltpu.SemaphoreType.DMA((5 * views + FAR + WIDE + 16,)),
+            pltpu.SemaphoreType.DMA((5 * views + 2 * FAR + 2 * WIDE + 16,)),
+            pltpu.SemaphoreType.DMA((5 * views + 2 * FAR + 2 * WIDE + 16,)),
             *[numbers(1, 1)] * (2 * (4 + 2 * rounds)),
         ],
         compiler_params=pltpu.CompilerParams(

time: 94.3 us -> 93.5 us (level)
  the two profiles are of different devices: /device:TPU:0 before, /device:TPU:1 now
where the time goes in v8:
time: 93.5 us; the launch traced here: 93.4 us
  Pallas kernels  89.2 us (95%)
  local copies, waits for them, and re-layouts  2.92 us (3%)
  between operations  1.28 us (1%)
    pallas_call x1, Pallas kernels, quick(): pl.pallas_call(functools.partial(quick_kernel, degree), out_shape=(jax.Sh...  89.2 us
    unnamed x8, local copies, waits for them, and re-layouts  2.92 us

profile of v8, /device:TPU:1, one launch (start us, length us, event | category | flops | bytes accessed | tf_op | source)
XLA Modules:
  0.0 93.4 jit_solution(4799053771658712179)
XLA Ops:
  0.7 0.0 copy-start.1
  0.7 0.0 copy-start.2
  0.7 1.4 %copy.11.refs_3_ = bf16[4,196,768]{2,1,0:T(8,128)(2,1)S(1)} copy(bf16[4,196,768]{2,0,1:T(4,128)(2,1)} %param.10) | data formatting | bytes 2408448 | tf_op args[0]
  2.1 0.0 copy-done.1
  2.1 0.0 copy-done.2
  2.1 0.0 copy-start
  2.1 89.2 %sublayer_quick.1 = (bf16[4,196,768]{2,1,0:T(8,128)(2,1)S(1)}, s32[1,1]{1,0:T(1,128)}) custom-call(s32[4,4]{1,0:T(4,128)S(1)} %copy-done.1, s32[4]{0:T(128)S(1)} %copy-done.2, s32[1]{0:T(128)S(6)} %copy.16.refs_2_, bf16[4,196,768]{2,1,0:T(8,128)(2,1)S(1)} %copy.11.refs_3_, bf16[768,768]{1,0:T(8,128)(2,1)} %refs_4_.1, bf16[768,768]{1,0:T(8,128)(2,1)} %refs_5_.1, ...), custom_call_target="tpu_custom_call" | custom-call | tf_op jit(solution)/shard_map/sublayer_quick/pallas_call | solution.py:975
  91.8 0.0 copy-done
  91.9 1.5 %copy.13 = bf16[4,196,768]{2,0,1:T(4,128)(2,1)} copy(bf16[4,196,768]{2,1,0:T(8,128)(2,1)S(1)} %get-tuple-element.37) | data formatting | bytes 2408448
  (1 shorter events, 0.0 us)
Async XLA Ops:
  0.7 1.4 %copy-start.1 = (s32[4,4]{1,0:T(4,128)S(1)}, s32[4,4]{1,0:T(4,128)}, u32[]{:S(2)}) copy-start(s32[4,4]{1,0:T(4,128)} %refs_0_.1) | copy-start | bytes 196
  0.7 1.4 %copy-start.2 = (s32[4]{0:T(128)S(1)}, s32[4]{0:T(128)}, u32[]{:S(2)}) copy-start(s32[4]{0:T(128)} %refs_1_.1) | copy-start | bytes 52
  2.1 89.7 %copy-start = (bf16[4,196,768]{2,0,1:T(4,128)(2,1)S(1)}, bf16[4,196,768]{2,0,1:T(4,128)(2,1)}, u32[]{:S(2)}) copy-start(bf16[4,196,768]{2,0,1:T(4,128)(2,1)} %param.10) | copy-start | bytes 3612676

commit v9 on v8

--- a/solution.py
+++ b/solution.py
@@ -803,6 +803,7 @@
             cell = jnp.where(match, codes[0, e], cell)
             view = jnp.where(match, e // degree, view)
         source = jnp.where(cell < 0, KEYS, sources[0, jnp.maximum(cell, 0)])
+        source = jnp.clip(source, 0, KEYS + 1)
         table[1, r], table[2, r] = jnp.where(r < 2, KEYS + r, source), view
         return carry
 
@@ -865,6 +866,7 @@
             learn([KEYS, KEYS + 1], 2)
         if v == 1:
             attends(-2, 0)
+            results[0] = results[0] + results[1]
     bounds = [max(0, entries - n) for n in (15, 12, 9, 7, 6, 3, 0)]
     attends(0, bounds[0])
     inside = {3: (bounds[0], bounds[0] + 1), 5: (bounds[2] - 1, bounds[2]), 6: (bounds[3], bounds[4])}
@@ -905,7 +907,7 @@
     for v in range(views):
         is_key = (key_view == v).astype(jnp.int32)
         total = counts[v]
-        mixed = is_key.astype(jnp.float32) * (results[0] + results[1])
+        mixed = is_key.astype(jnp.float32) * results[0]
         for e in range(degree):
             live = (total > e).astype(jnp.int32).astype(jnp.float32)
             mixed += live * results[table[0, v * degree + e]]

time: 93.5 us -> 93.3 us (level)
  no operation moved by 1% of the time
where the time goes in v9:
time: 93.3 us; the launch traced here: 93.1 us
  Pallas kernels  88.9 us (95%)
  local copies, waits for them, and re-layouts  2.92 us (3%)
  between operations  1.28 us (1%)
    pallas_call x1, Pallas kernels, quick(): pl.pallas_call(functools.partial(quick_kernel, degree), out_shape=(jax.Sh...  88.9 us
    unnamed x8, local copies, waits for them, and re-layouts  2.92 us

profile of v9, /device:TPU:1, one launch (start us, length us, event | category | flops | bytes accessed | tf_op | source)
XLA Modules:
  0.0 93.1 jit_solution(17829474678702867775)
XLA Ops:
  0.7 0.0 copy-start.1
  0.7 0.0 copy-start.2
  0.7 1.4 %copy.11.refs_3_ = bf16[4,196,768]{2,1,0:T(8,128)(2,1)S(1)} copy(bf16[4,196,768]{2,0,1:T(4,128)(2,1)} %param.10) | data formatting | bytes 2408448 | tf_op args[0]
  2.1 0.0 copy-done.1
  2.1 0.0 copy-done.2
  2.1 0.0 copy-start
  2.1 88.9 %sublayer_quick.1 = (bf16[4,196,768]{2,1,0:T(8,128)(2,1)S(1)}, s32[1,1]{1,0:T(1,128)}) custom-call(s32[4,4]{1,0:T(4,128)S(1)} %copy-done.1, s32[4]{0:T(128)S(1)} %copy-done.2, s32[1]{0:T(128)S(6)} %copy.16.refs_2_, bf16[4,196,768]{2,1,0:T(8,128)(2,1)S(1)} %copy.11.refs_3_, bf16[768,768]{1,0:T(8,128)(2,1)} %refs_4_.1, bf16[768,768]{1,0:T(8,128)(2,1)} %refs_5_.1, ...), custom_call_target="tpu_custom_call" | custom-call | tf_op jit(solution)/shard_map/sublayer_quick/pallas_call | solution.py:977
  91.6 0.0 copy-done
  91.6 1.5 %copy.13 = bf16[4,196,768]{2,0,1:T(4,128)(2,1)} copy(bf16[4,196,768]{2,1,0:T(8,128)(2,1)S(1)} %get-tuple-element.37) | data formatting | bytes 2408448
  (1 shorter events, 0.0 us)
Async XLA Ops:
  0.7 1.4 %copy-start.1 = (s32[4,4]{1,0:T(4,128)S(1)}, s32[4,4]{1,0:T(4,128)}, u32[]{:S(2)}) copy-start(s32[4,4]{1,0:T(4,128)} %refs_0_.1) | copy-start | bytes 196
  0.7 1.4 %copy-start.2 = (s32[4]{0:T(128)S(1)}, s32[4]{0:T(128)}, u32[]{:S(2)}) copy-start(s32[4]{0:T(128)} %refs_1_.1) | copy-start | bytes 52
  2.1 89.5 %copy-start = (bf16[4,196,768]{2,0,1:T(4,128)(2,1)S(1)}, bf16[4,196,768]{2,0,1:T(4,128)(2,1)}, u32[]{:S(2)}) copy-start(bf16[4,196,768]{2,0,1:T(4,128)(2,1)} %param.10) | copy-start | bytes 3612676
